TPU v7x, 512 devices: a whole 4x8x8 slice. The times are simulated.
512 devices in a mesh: rows: 16 (over x_lo, z), cols: 32 (over y, x_hi, core).
Axes of the slice: x: 4 (x_hi: 2, x_lo: 2; x = x_hi * 2 + x_lo), y: 8, z: 8, core: 2. Of those that a mesh axis runs over, the one named last changes fastest.
Arguments:
- tokens: bfloat16 [128, 1024, 192], P('rows', 'cols'), may hold values from -60 to 60
- region_ids: int32 [128, 1024], P('rows', 'cols'), may hold values from 0 to 2
- upper_rim: bfloat16 [4, 1024, 192], P(None, 'cols'), may hold values from -60 to 60
- upper_ids: int32 [4, 1024], P(None, 'cols'), may hold values from 0 to 2
- lower_rim: bfloat16 [4, 1024, 192], P(None, 'cols'), may hold values from -60 to 60
- lower_ids: int32 [4, 1024], P(None, 'cols'), may hold values from 0 to 2
- cotangent: bfloat16 [128, 1024, 192], P('rows', 'cols'), may hold values from -6 to 6
- qkv_weight: bfloat16 [2, 192, 576], replicated, may hold values from -0.4375 to 0.4375
- proj_weight: bfloat16 [2, 192, 192], replicated, may hold values from -0.4375 to 0.4375
- inner_weight: bfloat16 [2, 192, 768], replicated, may hold values from -0.4375 to 0.4375
- outer_weight: bfloat16 [2, 768, 192], replicated, may hold values from -0.21875 to 0.21875
- bias_table: float32 [2, 225, 6], replicated, may hold values from -4 to 400
Outputs:
- token_grad: bfloat16 [128, 1024, 192], P('rows', 'cols')
- qkv_grad: float32 [2, 192, 576], P(None, 'rows', 'cols')
- proj_grad: float32 [2, 192, 192], P(None, 'rows', 'cols')
- inner_grad: float32 [2, 192, 768], P(None, 'rows', 'cols')
- outer_grad: float32 [2, 768, 192], P(None, 'rows', 'cols')
- table_grad: float32 [2, 225, 6], replicated
All inputs are finite; a program needn't handle non-finite values.
Results may differ from a plain program's by a relative error of at most 0.03.
Values may be sent and summed in bfloat16 or wider, within the bound.
A program may use at most 64 MiB of HBM per device.

v0:
```python
import jax
import jax.numpy as jnp
from jax import lax
from jax.sharding import PartitionSpec as P

WIN = 8
HALF = 4
BIAS_LEN = 225


EPS = 1e-05
MASKED = -1000000000.0


def with_halo(block, sides, width, periodic):
    for axis, dim in sides:
        count = lax.axis_size(axis)
        forward = [(i, i + 1) for i in range(count - 1)]
        if periodic:
            forward.append((count - 1, 0))
        backward = [(target, source) for source, target in forward]
        low = lax.ppermute(
            lax.slice_in_dim(block, block.shape[dim] - width, None, axis=dim), axis, forward
        )
        high = lax.ppermute(lax.slice_in_dim(block, 0, width, axis=dim), axis, backward)
        block = jnp.concatenate([low, block, high], axis=dim)
    return block


def normalize(values):
    center = jnp.mean(values, axis=-1, keepdims=True)
    shifted = values - center
    spread = jnp.mean(shifted * shifted, axis=-1, keepdims=True)
    return shifted * lax.rsqrt(spread + EPS)


def norm_back(source, grad_norm):
    _, pullback = jax.vjp(normalize, source.astype(jnp.float32))
    return pullback(grad_norm)[0]


def by_transpose(left, right):
    return lax.dot_general(
        left, right, (((1,), (1,)), ((), ())), preferred_element_type=jnp.float32
    )


def over_rows(left, right):
    return lax.dot_general(
        left, right, (((0,), (0,)), ((), ())), preferred_element_type=jnp.float32
    )


def windows(surface):
    grid_rows, grid_cols = (surface.shape[0], surface.shape[1])
    trailing = surface.shape[2:]
    blocked = surface.reshape((grid_rows // WIN, WIN, grid_cols // WIN, WIN) + trailing)
    permute = (0, 2, 1, 3) + tuple(range(4, 4 + len(trailing)))
    return blocked.transpose(permute).reshape(
        (grid_rows // WIN * (grid_cols // WIN), WIN * WIN) + trailing
    )


def unwindows(framed, grid_rows, grid_cols):
    trailing = framed.shape[2:]
    blocked = framed.reshape((grid_rows // WIN, grid_cols // WIN, WIN, WIN) + trailing)
    permute = (0, 2, 1, 3) + tuple(range(4, 4 + len(trailing)))
    return blocked.transpose(permute).reshape((grid_rows, grid_cols) + trailing)


def relative_onehot():
    places = jnp.arange(WIN * WIN, dtype=jnp.int32)
    pos_row = places // WIN
    pos_col = places % WIN
    lookup = (
        (pos_row[:, None] - pos_row[None, :] + WIN - 1) * (2 * WIN - 1)
        + pos_col[:, None]
        - pos_col[None, :]
        + WIN
        - 1
    )
    return (lookup[:, :, None] == jnp.arange(BIAS_LEN, dtype=jnp.int32)[None, None, :]).astype(
        jnp.float32
    )


def attend(normed_win, ids_win, qkv_weight, pos_bias):
    window_count, window_size, channels = normed_win.shape
    head_count = pos_bias.shape[0]
    head_size = channels // head_count
    score_scale = head_size ** (-0.5)
    qkv_all = jnp.dot(
        normed_win.reshape(window_count * window_size, channels),
        qkv_weight,
        preferred_element_type=jnp.float32,
    )
    qkv_all = qkv_all.astype(jnp.bfloat16).reshape(
        window_count, window_size, 3, head_count, head_size
    )
    scores = jnp.einsum(
        "nqhd,nkhd->nhqk", qkv_all[:, :, 0], qkv_all[:, :, 1], preferred_element_type=jnp.float32
    )
    scores = scores * score_scale + pos_bias[None]
    same_region = ids_win[:, :, None] == ids_win[:, None, :]
    scores = jnp.where(same_region[:, None], scores, MASKED)
    row_max = jnp.max(scores, axis=-1, keepdims=True)
    exponent = jnp.exp(scores - row_max)
    attn_probs = exponent / jnp.sum(exponent, axis=-1, keepdims=True)
    attn_out = jnp.einsum(
        "nhqk,nkhd->nqhd",
        attn_probs.astype(jnp.bfloat16),
        qkv_all[:, :, 2],
        preferred_element_type=jnp.float32,
    )
    return (
        qkv_all,
        attn_probs,
        attn_out.astype(jnp.bfloat16).reshape(window_count, window_size, channels),
    )


def attend_back(normed_win, qkv_all, attn_probs, grad_out, qkv_weight):
    window_count, window_size, channels = normed_win.shape
    head_count, head_size = (qkv_all.shape[3], qkv_all.shape[4])
    score_scale = head_size ** (-0.5)
    grad_heads = grad_out.reshape(window_count, window_size, head_count, head_size)
    grad_probs = jnp.einsum(
        "nqhd,nkhd->nhqk", grad_heads, qkv_all[:, :, 2], preferred_element_type=jnp.float32
    )
    grad_scores = attn_probs * (
        grad_probs - jnp.sum(grad_probs * attn_probs, axis=-1, keepdims=True)
    )
    grad_bias = jnp.sum(grad_scores, axis=0)
    scores_low = grad_scores.astype(jnp.bfloat16)
    grad_query = (
        jnp.einsum(
            "nhqk,nkhd->nqhd", scores_low, qkv_all[:, :, 1], preferred_element_type=jnp.float32
        )
        * score_scale
    )
    grad_key = (
        jnp.einsum(
            "nhqk,nqhd->nkhd", scores_low, qkv_all[:, :, 0], preferred_element_type=jnp.float32
        )
        * score_scale
    )
    grad_value = jnp.einsum(
        "nhqk,nqhd->nkhd",
        attn_probs.astype(jnp.bfloat16),
        grad_heads,
        preferred_element_type=jnp.float32,
    )
    grad_qkv = jnp.stack([grad_query, grad_key, grad_value], axis=2).astype(jnp.bfloat16)
    grad_qkv = grad_qkv.reshape(window_count * window_size, 3 * channels)
    flattened = normed_win.reshape(window_count * window_size, channels)
    grad_norm = by_transpose(grad_qkv, qkv_weight)
    grad_weight = over_rows(flattened, grad_qkv)
    return (grad_norm.reshape(window_count, window_size, channels), grad_weight, grad_bias)


def mixer_forward(surface, region, qkv_weight, table):
    grid_rows, grid_cols = (surface.shape[0], surface.shape[1])
    normed = normalize(surface.astype(jnp.float32)).astype(jnp.bfloat16)
    pos_bias = jnp.einsum("ijb,bh->hij", relative_onehot(), table, precision=lax.Precision.HIGHEST)
    qkv_all, attn_probs, attn_out = attend(windows(normed), windows(region), qkv_weight, pos_bias)
    return (normed, qkv_all, attn_probs, unwindows(attn_out, grid_rows, grid_cols))


def mixer_backward(surface, normed, qkv_all, attn_probs, grad_mix, qkv_weight):
    grid_rows, grid_cols = (surface.shape[0], surface.shape[1])
    grad_norm, grad_weight, grad_bias = attend_back(
        windows(normed), qkv_all, attn_probs, windows(grad_mix), qkv_weight
    )
    grad_surface = norm_back(surface, unwindows(grad_norm, grid_rows, grid_cols))
    grad_table = jnp.einsum(
        "ijb,hij->bh", relative_onehot(), grad_bias, precision=lax.Precision.HIGHEST
    )
    return (grad_surface, grad_weight, grad_table)


def channel_forward(middle, inner_w, outer_w):
    normed = normalize(middle.astype(jnp.float32)).astype(jnp.bfloat16)
    hidden_pre = jnp.dot(normed, inner_w, preferred_element_type=jnp.float32)
    hidden_act = jax.nn.gelu(hidden_pre, approximate=False).astype(jnp.bfloat16)
    output = (
        middle.astype(jnp.float32)
        + jnp.dot(hidden_act, outer_w, preferred_element_type=jnp.float32)
    ).astype(jnp.bfloat16)
    return (normed, hidden_pre, hidden_act, output)


def channel_backward(middle, normed, hidden_pre, hidden_act, grad_out, inner_w, outer_w):
    grad_act = by_transpose(grad_out, outer_w)
    grad_outer = over_rows(hidden_act, grad_out)
    _, pullback = jax.vjp(lambda inputs: jax.nn.gelu(inputs, approximate=False), hidden_pre)
    grad_pre = pullback(grad_act)[0].astype(jnp.bfloat16)
    grad_norm = by_transpose(grad_pre, inner_w)
    grad_inner = over_rows(normed, grad_pre)
    grad_middle = (grad_out.astype(jnp.float32) + norm_back(middle, grad_norm)).astype(jnp.bfloat16)
    return (grad_middle, grad_inner, grad_outer)


def fold_rims(grad_ext):
    col_edges = jnp.concatenate([grad_ext[:, :HALF], grad_ext[:, -HALF:]], axis=1)
    col_recv = with_halo(col_edges.astype(jnp.bfloat16), (("cols", 1),), HALF, True).astype(
        col_edges.dtype
    )
    center = grad_ext[:, HALF:-HALF]
    center = jnp.concatenate(
        [
            center[:, :HALF] + col_recv[:, :HALF],
            center[:, HALF:-HALF],
            center[:, -HALF:] + col_recv[:, -HALF:],
        ],
        axis=1,
    )
    row_edges = jnp.concatenate([center[:HALF], center[-HALF:]], axis=0)
    row_recv = with_halo(row_edges.astype(jnp.bfloat16), (("rows", 0),), HALF, False).astype(
        row_edges.dtype
    )
    interior = center[HALF:-HALF]
    return jnp.concatenate(
        [
            interior[:HALF] + row_recv[:HALF],
            interior[HALF:-HALF],
            interior[-HALF:] + row_recv[-HALF:],
        ],
        axis=0,
    )


def reduce_grads(qkv_term, proj_term, inner_term, outer_term):
    row_count = lax.axis_size("rows")
    col_count = lax.axis_size("cols")
    tile_count = row_count * col_count
    reduced = (
        lax.psum_scatter(
            qkv_term.astype(jnp.bfloat16), "cols", scatter_dimension=1, tiled=True
        ).astype(jnp.float32),
        lax.psum_scatter(
            proj_term.astype(jnp.bfloat16), "cols", scatter_dimension=1, tiled=True
        ).astype(jnp.float32),
        lax.psum_scatter(
            inner_term.astype(jnp.bfloat16), "cols", scatter_dimension=1, tiled=True
        ).astype(jnp.float32),
        lax.psum_scatter(
            outer_term.astype(jnp.bfloat16), "cols", scatter_dimension=1, tiled=True
        ).astype(jnp.float32),
    )
    reduced = (
        lax.psum_scatter(
            reduced[0].astype(jnp.bfloat16), "rows", scatter_dimension=0, tiled=True
        ).astype(jnp.float32),
        lax.psum_scatter(
            reduced[1].astype(jnp.bfloat16), "rows", scatter_dimension=0, tiled=True
        ).astype(jnp.float32),
        lax.psum_scatter(
            reduced[2].astype(jnp.bfloat16), "rows", scatter_dimension=0, tiled=True
        ).astype(jnp.float32),
        lax.psum_scatter(
            reduced[3].astype(jnp.bfloat16), "rows", scatter_dimension=0, tiled=True
        ).astype(jnp.float32),
    )
    return tuple((section / tile_count for section in reduced))


def local(
    tokens,
    region_ids,
    upper_rim,
    upper_ids,
    lower_rim,
    lower_ids,
    cotangent,
    qkv_weight,
    proj_weight,
    inner_weight,
    outer_weight,
    bias_table,
):
    tile_rows, tile_cols, channels = tokens.shape
    row_index = lax.axis_index("rows")
    row_count = lax.axis_size("rows")
    tile_count = row_count * lax.axis_size("cols")
    normed_one, qkv_one, probs_one, mix_one = mixer_forward(
        tokens, region_ids, qkv_weight[0], bias_table[0]
    )
    mix_flat_one = mix_one.reshape(tile_rows * tile_cols, channels)
    middle_one = (
        tokens.reshape(-1, channels).astype(jnp.float32)
        + jnp.dot(mix_flat_one, proj_weight[0], preferred_element_type=jnp.float32)
    ).astype(jnp.bfloat16)
    chan_one = channel_forward(middle_one, inner_weight[0], outer_weight[0])
    first_out = chan_one[3].reshape(tile_rows, tile_cols, channels)
    region_low = region_ids.astype(jnp.bfloat16)
    row_ext, row_ids = (
        with_halo(first_out, (("rows", 0),), HALF, False),
        with_halo(region_low, (("rows", 0),), HALF, False),
    )
    at_top = row_index == 0
    at_bottom = row_index == row_count - 1
    row_ext = jnp.concatenate(
        [
            jnp.where(at_top, upper_rim, row_ext[:HALF]),
            row_ext[HALF:-HALF],
            jnp.where(at_bottom, lower_rim, row_ext[-HALF:]),
        ],
        axis=0,
    )
    row_ids = jnp.concatenate(
        [
            jnp.where(at_top, upper_ids.astype(jnp.bfloat16), row_ids[:HALF]),
            row_ids[HALF:-HALF],
            jnp.where(at_bottom, lower_ids.astype(jnp.bfloat16), row_ids[-HALF:]),
        ],
        axis=0,
    )
    extended, ext_ids = (
        with_halo(row_ext, (("cols", 1),), HALF, True),
        with_halo(row_ids, (("cols", 1),), HALF, True),
    )
    ext_region = ext_ids.astype(jnp.int32)
    normed_two, qkv_two, probs_two, mix_ext = mixer_forward(
        extended, ext_region, qkv_weight[1], bias_table[1]
    )
    mix_flat_two = mix_ext[HALF : HALF + tile_rows, HALF : HALF + tile_cols].reshape(
        tile_rows * tile_cols, channels
    )
    middle_two = (
        chan_one[3].astype(jnp.float32)
        + jnp.dot(mix_flat_two, proj_weight[1], preferred_element_type=jnp.float32)
    ).astype(jnp.bfloat16)
    chan_two = channel_forward(middle_two, inner_weight[1], outer_weight[1])
    grad_out = cotangent.reshape(-1, channels)
    grad_mid_two, inner_two, outer_two = channel_backward(
        middle_two,
        chan_two[0],
        chan_two[1],
        chan_two[2],
        grad_out,
        inner_weight[1],
        outer_weight[1],
    )
    proj_two = over_rows(mix_flat_two, grad_mid_two)
    grad_mix_two = (
        by_transpose(grad_mid_two, proj_weight[1])
        .astype(jnp.bfloat16)
        .reshape(tile_rows, tile_cols, channels)
    )
    grad_mix_ext = jnp.pad(grad_mix_two, ((HALF, HALF), (HALF, HALF), (0, 0)))
    grad_ext, qkv_two_grad, table_two = mixer_backward(
        extended, normed_two, qkv_two, probs_two, grad_mix_ext, qkv_weight[1]
    )
    folded = fold_rims(grad_ext)
    grad_first = (
        grad_mid_two.reshape(tile_rows, tile_cols, channels).astype(jnp.float32) + folded
    ).astype(jnp.bfloat16)
    summed_two = reduce_grads(qkv_two_grad, proj_two, inner_two, outer_two)
    grad_mid_one, inner_one, outer_one = channel_backward(
        middle_one,
        chan_one[0],
        chan_one[1],
        chan_one[2],
        grad_first.reshape(-1, channels),
        inner_weight[0],
        outer_weight[0],
    )
    proj_one = over_rows(mix_flat_one, grad_mid_one)
    grad_mix_one = (
        by_transpose(grad_mid_one, proj_weight[0])
        .astype(jnp.bfloat16)
        .reshape(tile_rows, tile_cols, channels)
    )
    grad_tokens, qkv_one_grad, table_one = mixer_backward(
        tokens, normed_one, qkv_one, probs_one, grad_mix_one, qkv_weight[0]
    )
    token_grad = (
        grad_mid_one.reshape(tile_rows, tile_cols, channels).astype(jnp.float32) + grad_tokens
    ).astype(jnp.bfloat16)
    summed_one = reduce_grads(qkv_one_grad, proj_one, inner_one, outer_one)
    table_sum = lax.psum(jnp.stack([table_one, table_two]), ("rows", "cols"))
    qkv_grad = jnp.stack([summed_one[0], summed_two[0]])
    proj_grad = jnp.stack([summed_one[1], summed_two[1]])
    inner_grad = jnp.stack([summed_one[2], summed_two[2]])
    outer_grad = jnp.stack([summed_one[3], summed_two[3]])
    return (token_grad, qkv_grad, proj_grad, inner_grad, outer_grad, table_sum / tile_count)


def solution(mesh):
    return jax.shard_map(
        local,
        mesh=mesh,
        in_specs=(
            P("rows", "cols", None),
            P("rows", "cols"),
            P(None, "cols", None),
            P(None, "cols"),
            P(None, "cols", None),
            P(None, "cols"),
            P("rows", "cols", None),
            P(),
            P(),
            P(),
            P(),
            P(),
        ),
        out_specs=(
            P("rows", "cols", None),
            P(None, "rows", "cols"),
            P(None, "rows", "cols"),
            P(None, "rows", "cols"),
            P(None, "rows", "cols"),
            P(),
        ),
        check_vma=False,
    )
```

profile of v0, /device:TPU:4, one launch (start us, length us, event | category | flops | bytes accessed | tf_op | source)
XLA Modules:
  0.0 740.5 jit_solution(4633801604680968060)
XLA Ops:
  8.5 4.8 collective-permute-start.4
  33.3 5.2 collective-permute-start
  44.7 5.1 collective-permute-start.7
  51.7 4.4 collective-permute-start.2
  92.6 4.0 copy.147
  96.6 5.6 convert_element_type.304
  113.6 5.3 collective-permute-start.8
  122.7 4.7 collective-permute-start.10
  129.3 5.8 collective-permute-done.11
  143.4 80.5 %fusion.122 = (bf16[192,24]{0,1:T(8,128)(2,1)S(1)}, bf16[192,24]{0,1:T(8,128)(2,1)S(1)}, bf16[192,8]{0,1:T(8,128)(2,1)S(1)}, bf16[192,8]{0,1:T(8,128)(2,1)S(1)},...) fusion(bf16[192,576]{0,1:T(8,128)(2,1)} %convolution_convert_fusion.9, ...), kind=kCustom, calls=%all-reduce-scatter.6 | all-reduce-scatter fusion | flops 786434 | bytes 1230848
  225.3 8.8 %collective-permute-start.50 = (bf16[768,8]{0,1:T(8,128)(2,1)S(1)}, bf16[768,8]{0,1:T(8,128)(2,1)S(1)}, u32[]{:S(2)}, u32[]{:S(2)}) collective-permute-start(bf16[768,8]{0,1:T(8,128)(2,1)S(1)} %get-tuple-element.41), channel_id=1, source_target_pairs={{0,7},{1,8},{2,9},{3,10},{4,11},{5,12},{6,13},{7,14},{8,15},{9,16}... | collective-permute-start | bytes 36872
  234.1 7.5 %collective-permute-start.49 = (bf16[768,8]{0,1:T(8,128)(2,1)S(1)}, bf16[768,8]{0,1:T(8,128)(2,1)S(1)}, u32[]{:S(2)}, u32[]{:S(2)}) collective-permute-start(bf16[768,8]{0,1:T(8,128)(2,1)S(1)} %get-tuple-element.41), channel_id=1, source_target_pairs={{0,6},{1,7},{2,8},{3,9},{4,10},{5,11},{6,12},{7,13},{8,14},{9,15},... | collective-permute-start | bytes 36872
  244.2 5.9 collective-permute-start.46
  270.4 4.5 collective-permute-start.54
  289.9 4.1 collective-permute-start.41
  306.2 4.0 collective-permute-start.38
  323.2 103.0 %psum.7 = f32[2,225,6]{1,2,0:T(8,128)S(1)} all-reduce(f32[2,225,6]{1,2,0:T(8,128)S(1)} %pad_maximum_fusion.16), channel_id=1, replica_groups=mesh['rows'=16,'cols'=32] {'rows','cols'}, use_global_device_ids=true, to_apply=%region_40.41 | all-reduce | flops 2700 | bytes 21600 | tf_op jit(solution)/shard_map/psum | solution.py:381
  437.9 4.6 collective-permute-start.27
  444.0 4.6 collective-permute-start.26
  448.6 5.2 collective-permute-start.25
  478.9 4.3 collective-permute-start.14
  495.3 49.6 %reduce-scatter.29.cloned.1.call-done = bf16[192,24]{0,1:T(8,128)(2,1)} async-done(((bf16[192,768]{0,1:T(8,128)(2,1)}), bf16[192,24]{0,1:T(8,128)(2,1)}) %reduce-scatter.29.cloned.1.call-update) | async-done | bytes 9232 | tf_op jit(solution)/shard_map/reduce_scatter | solution.py:243
  545.0 121.3 %reduce-scatter.27.cloned.1.call-done = bf16[192,24]{0,1:T(8,128)(2,1)} async-done(((bf16[192,768]{0,1:T(8,128)(2,1)}), bf16[192,24]{0,1:T(8,128)(2,1)}) %reduce-scatter.27.cloned.1.call-update) | async-done | bytes 9232 | tf_op jit(solution)/shard_map/reduce_scatter | solution.py:243
  666.3 65.0 %all-reduce.19 = (bf16[192,18]{0,1:T(8,128)(2,1)S(1)}, bf16[192,18]{0,1:T(8,128)(2,1)S(1)}, bf16[192,6]{0,1:T(8,128)(2,1)S(1)}, bf16[192,6]{0,1:T(8,128)(2,1)S(1...) all-reduce(bf16[192,18]{0,1:T(8,128)(2,1)S(1)} %constant_dynamic-sl, ...), channel_id=5, replica_groups=mesh['rows'=16,'cols'=32] {'rows'}, use_global_device_ids=true, to_apply=%region_25.26.clone | all-reduce | flops 18432 | bytes 73728
  (456 shorter events, 203.9 us)
Async XLA Ops:
  7.2 485.9 %reduce-scatter.31.cloned.1.call-start = ((), (), s32[]{:S(2)}) async-start(), calls=%async_computation.6 | async-start | bytes 208896
  8.5 33.5 %collective-permute-start.4 = (bf16[4,32]{1,0:T(4,128)(2,1)}, bf16[4,32]{1,0:T(4,128)(2,1)}, u32[]{:S(2)}, u32[]{:S(2)}) collective-permute-start(bf16[4,32]{1,0:T(4,128)(2,1)} %get-tuple-element.76), channel_id=1, source_target_pairs={{0,32},{32,64},{64,96},{96,128},{128,160},{160,192},{192,224},{224... | collective-permute-start | bytes 776 | tf_op jit(solution)/shard_map/ppermute | solution.py:22
  13.4 28.6 %collective-permute-start.5 = (bf16[4,32]{1,0:T(4,128)(2,1)}, bf16[4,32]{1,0:T(4,128)(2,1)}, u32[]{:S(2)}, u32[]{:S(2)}) collective-permute-start(bf16[4,32]{1,0:T(4,128)(2,1)} %get-tuple-element.77), channel_id=1, source_target_pairs={{32,0},{64,32},{96,64},{128,96},{160,128},{192,160},{224,192},{256... | collective-permute-start | bytes 776 | tf_op jit(solution)/shard_map/ppermute | solution.py:25
  31.9 19.7 %collective-permute-start.1 = (bf16[4,32,192]{2,1,0:T(8,128)(2,1)S(1)}, bf16[4,32,192]{2,1,0:T(8,128)(2,1)S(1)}, u32[]{:S(2)}, u32[]{:S(2)}) collective-permute-start(bf16[4,32,192]{2,1,0:T(8,128)(2,1)S(1)} %bitcast.340), channel_id=1, source_target_pairs={{32,0},{64,32},{96,64},{128,96},{160,128},{192,160},{224,192},{256... | collective-permute-start | bytes 147464 | tf_op jit(solution)/shard_map/ppermute | solution.py:25
  224.0 20.2 %collective-permute-start.51 = (bf16[768,6]{0,1:T(8,128)(2,1)S(1)}, bf16[768,6]{0,1:T(8,128)(2,1)S(1)}, u32[]{:S(2)}, u32[]{:S(2)}) collective-permute-start(bf16[768,6]{0,1:T(8,128)(2,1)S(1)} %slice.212), channel_id=1, source_target_pairs={{0,8},{1,9},{2,10},{3,11},{4,12},{5,13},{6,14},{7,15},{8,16},{9,17... | collective-permute-start | bytes 27656
  225.3 29.3 %collective-permute-start.50 = (bf16[768,8]{0,1:T(8,128)(2,1)S(1)}, bf16[768,8]{0,1:T(8,128)(2,1)S(1)}, u32[]{:S(2)}, u32[]{:S(2)}) collective-permute-start(bf16[768,8]{0,1:T(8,128)(2,1)S(1)} %get-tuple-element.41), channel_id=1, source_target_pairs={{0,7},{1,8},{2,9},{3,10},{4,11},{5,12},{6,13},{7,14},{8,15},{9,16}... | collective-permute-start | bytes 36872
  234.1 21.8 %collective-permute-start.49 = (bf16[768,8]{0,1:T(8,128)(2,1)S(1)}, bf16[768,8]{0,1:T(8,128)(2,1)S(1)}, u32[]{:S(2)}, u32[]{:S(2)}) collective-permute-start(bf16[768,8]{0,1:T(8,128)(2,1)S(1)} %get-tuple-element.41), channel_id=1, source_target_pairs={{0,6},{1,7},{2,8},{3,9},{4,10},{5,11},{6,12},{7,13},{8,14},{9,15},... | collective-permute-start | bytes 36872
  254.6 20.3 %collective-permute-start.58 = (bf16[768,8]{0,1:T(8,128)(2,1)S(1)}, bf16[768,8]{0,1:T(8,128)(2,1)S(1)}, u32[]{:S(2)}, u32[]{:S(2)}) collective-permute-start(bf16[768,8]{0,1:T(8,128)(2,1)S(1)} %get-tuple-element.40), channel_id=1, source_target_pairs={{0,7},{1,8},{2,9},{3,10},{4,11},{5,12},{6,13},{7,14},{8,15},{9,16}... | collective-permute-start | bytes 36872
  255.9 21.2 %collective-permute-start.57 = (bf16[768,8]{0,1:T(8,128)(2,1)S(1)}, bf16[768,8]{0,1:T(8,128)(2,1)S(1)}, u32[]{:S(2)}, u32[]{:S(2)}) collective-permute-start(bf16[768,8]{0,1:T(8,128)(2,1)S(1)} %get-tuple-element.40), channel_id=1, source_target_pairs={{0,6},{1,7},{2,8},{3,9},{4,10},{5,11},{6,12},{7,13},{8,14},{9,15},... | collective-permute-start | bytes 36872
  280.0 214.0 %reduce-scatter.33.cloned.1.call-start = ((), (), s32[]{:S(2)}) async-start(), calls=%async_computation.7 | async-start | bytes 208896
  285.5 259.5 %reduce-scatter.29.cloned.1.call-start = ((), (), s32[]{:S(2)}) async-start(), calls=%async_computation.5 | async-start | bytes 405504 | tf_op jit(solution)/shard_map/reduce_scatter | solution.py:243
  287.2 379.1 %reduce-scatter.27.cloned.1.call-start = ((), (), s32[]{:S(2)}) async-start(), calls=%async_computation.4 | async-start | bytes 405504 | tf_op jit(solution)/shard_map/reduce_scatter | solution.py:243
  288.4 21.7 %collective-permute-start.42 = (bf16[192,8]{0,1:T(8,128)(2,1)S(1)}, bf16[192,8]{0,1:T(8,128)(2,1)S(1)}, u32[]{:S(2)}, u32[]{:S(2)}) collective-permute-start(bf16[192,8]{0,1:T(8,128)(2,1)S(1)} %get-tuple-element.38), channel_id=1, source_target_pairs={{0,7},{1,8},{2,9},{3,10},{4,11},{5,12},{6,13},{7,14},{8,15},{9,16}... | collective-permute-start | bytes 9224
  289.9 23.8 %collective-permute-start.41 = (bf16[192,8]{0,1:T(8,128)(2,1)S(1)}, bf16[192,8]{0,1:T(8,128)(2,1)S(1)}, u32[]{:S(2)}, u32[]{:S(2)}) collective-permute-start(bf16[192,8]{0,1:T(8,128)(2,1)S(1)} %get-tuple-element.38), channel_id=1, source_target_pairs={{0,6},{1,7},{2,8},{3,9},{4,10},{5,11},{6,12},{7,13},{8,14},{9,15},... | collective-permute-start | bytes 9224
  294.0 21.6 %collective-permute-start.40 = (bf16[192,8]{0,1:T(8,128)(2,1)S(1)}, bf16[192,8]{0,1:T(8,128)(2,1)S(1)}, u32[]{:S(2)}, u32[]{:S(2)}) collective-permute-start(bf16[192,8]{0,1:T(8,128)(2,1)S(1)} %get-tuple-element.38), channel_id=1, source_target_pairs={{0,5},{1,6},{2,7},{3,8},{4,9},{5,10},{6,11},{7,12},{8,13},{9,14},{... | collective-permute-start | bytes 9224
  310.2 116.1 %collective-permute-start.37 = (bf16[192,8]{0,1:T(8,128)(2,1)S(1)}, bf16[192,8]{0,1:T(8,128)(2,1)S(1)}, u32[]{:S(2)}, u32[]{:S(2)}) collective-permute-start(bf16[192,8]{0,1:T(8,128)(2,1)S(1)} %get-tuple-element.38), channel_id=1, source_target_pairs={{0,2},{1,3},{2,4},{3,5},{4,6},{5,7},{6,8},{7,9},{8,10},{9,11},{10,... | collective-permute-start | bytes 9224
  313.6 115.9 %collective-permute-start.36 = (bf16[192,8]{0,1:T(8,128)(2,1)S(1)}, bf16[192,8]{0,1:T(8,128)(2,1)S(1)}, u32[]{:S(2)}, u32[]{:S(2)}) collective-permute-start(bf16[192,8]{0,1:T(8,128)(2,1)S(1)} %get-tuple-element.38), channel_id=1, source_target_pairs={{0,1},{1,2},{2,3},{3,4},{4,5},{5,6},{6,7},{7,8},{8,9},{9,10},{10,1... | collective-permute-start | bytes 9224
  315.6 116.7 %collective-permute-start.34 = (bf16[192,8]{0,1:T(8,128)(2,1)S(1)}, bf16[192,8]{0,1:T(8,128)(2,1)S(1)}, u32[]{:S(2)}, u32[]{:S(2)}) collective-permute-start(bf16[192,8]{0,1:T(8,128)(2,1)S(1)} %get-tuple-element.39), channel_id=1, source_target_pairs={{0,7},{1,8},{2,9},{3,10},{4,11},{5,12},{6,13},{7,14},{8,15},{9,16}... | collective-permute-start | bytes 9224
  319.1 116.5 %collective-permute-start.33 = (bf16[192,8]{0,1:T(8,128)(2,1)S(1)}, bf16[192,8]{0,1:T(8,128)(2,1)S(1)}, u32[]{:S(2)}, u32[]{:S(2)}) collective-permute-start(bf16[192,8]{0,1:T(8,128)(2,1)S(1)} %get-tuple-element.39), channel_id=1, source_target_pairs={{0,6},{1,7},{2,8},{3,9},{4,10},{5,11},{6,12},{7,13},{8,14},{9,15},... | collective-permute-start | bytes 9224
  321.9 116.0 %collective-permute-start.32 = (bf16[192,8]{0,1:T(8,128)(2,1)S(1)}, bf16[192,8]{0,1:T(8,128)(2,1)S(1)}, u32[]{:S(2)}, u32[]{:S(2)}) collective-permute-start(bf16[192,8]{0,1:T(8,128)(2,1)S(1)} %get-tuple-element.39), channel_id=1, source_target_pairs={{0,5},{1,6},{2,7},{3,8},{4,9},{5,10},{6,11},{7,12},{8,13},{9,14},{... | collective-permute-start | bytes 9224
  432.3 21.5 %collective-permute-start.29 = (bf16[192,8]{0,1:T(8,128)(2,1)S(1)}, bf16[192,8]{0,1:T(8,128)(2,1)S(1)}, u32[]{:S(2)}, u32[]{:S(2)}) collective-permute-start(bf16[192,8]{0,1:T(8,128)(2,1)S(1)} %get-tuple-element.39), channel_id=1, source_target_pairs={{0,2},{1,3},{2,4},{3,5},{4,6},{5,7},{6,8},{7,9},{8,10},{9,11},{10,... | collective-permute-start | bytes 9224
  435.6 19.5 %collective-permute-start.28 = (bf16[192,8]{0,1:T(8,128)(2,1)S(1)}, bf16[192,8]{0,1:T(8,128)(2,1)S(1)}, u32[]{:S(2)}, u32[]{:S(2)}) collective-permute-start(bf16[192,8]{0,1:T(8,128)(2,1)S(1)} %get-tuple-element.39), channel_id=1, source_target_pairs={{0,1},{1,2},{2,3},{3,4},{4,5},{5,6},{6,7},{7,8},{8,9},{9,10},{10,1... | collective-permute-start | bytes 9224
  437.9 20.9 %collective-permute-start.27 = (bf16[192,18]{0,1:T(8,128)(2,1)S(1)}, bf16[192,18]{0,1:T(8,128)(2,1)S(1)}, u32[]{:S(2)}, u32[]{:S(2)}) collective-permute-start(bf16[192,18]{0,1:T(8,128)(2,1)S(1)} %slice.209), channel_id=1, source_target_pairs={{0,8},{1,9},{2,10},{3,11},{4,12},{5,13},{6,14},{7,15},{8,16},{9,17... | collective-permute-start | bytes 20744
  444.0 19.4 %collective-permute-start.26 = (bf16[192,24]{0,1:T(8,128)(2,1)S(1)}, bf16[192,24]{0,1:T(8,128)(2,1)S(1)}, u32[]{:S(2)}, u32[]{:S(2)}) collective-permute-start(bf16[192,24]{0,1:T(8,128)(2,1)S(1)} %get-tuple-element.36), channel_id=1, source_target_pairs={{0,7},{1,8},{2,9},{3,10},{4,11},{5,12},{6,13},{7,14},{8,15},{9,16}... | collective-permute-start | bytes 27656
  (112 other events, 1378.9 us)
Sparse Core Ops, SparseCore 0:
  280.1 74.2 reduce-scatter.30
  357.1 70.0 reduce-scatter.32
  431.8 113.1 reduce-scatter.28
  549.4 116.8 reduce-scatter.26
where the time goes:
time: 751 us; the launch traced here: 740 us
  blocking collectives  248 us (33%)
  waiting for transfers between devices  188 us (25%)
  starting transfers between devices  175 us (23%)
  local copies, waits for them, and re-layouts  55.5 us (7%)
  matrix products  40.7 us (5%)
  between operations  18.6 us (2%)
  other arithmetic  14.1 us (2%)
    reduce_scatter x2, waiting for transfers between devices, reduce_grads(): lax.psum_scatter(inner_term.astype(jnp.bfloat16), 'cols', scatter_dimensi...  171 us
    unnamed x2, blocking collectives  145 us
    unnamed x50, starting transfers between devices  135 us
    psum x1, blocking collectives, local(): table_sum = lax.psum(jnp.stack([table_one, table_two]), ('rows', 'cols'))  103 us
    ppermute x6, starting transfers between devices, with_halo(): lax.ppermute(lax.slice_in_dim(block, block.shape[dim] - width, None, axis...  26.4 us
    unnamed x173, local copies, waits for them, and re-layouts  19 us
  transfers between devices with their start and end apart: 64, of which 12 were waited for; matrix products, arithmetic and copies ran while one was open for 6% of the time, Pallas kernels for 0%

commit v1 on v0

v1 whole, which is shorter than its diff:
```python
import functools
import math
import types

import jax
import jax.numpy as jnp
from jax import lax
from jax.experimental import pallas as pl
from jax.experimental.pallas import tpu as pltpu
from jax.sharding import PartitionSpec as P

C = 192
HEADS = 6
HD = 32
HID = 768
WIN = 8
HALF = 4
EPS = 1e-05
MASKED = -1000000000.0
SCALE = HD**-0.5
CW = 256
CHUNK = 80
F32 = jnp.float32
BF16 = jnp.bfloat16
MESH = pl.DeviceIdType.MESH


def dot(a, b):
    return lax.dot_general(a, b, (((1,), (0,)), ((), ())), preferred_element_type=F32)


def dot_t(a, b):
    return lax.dot_general(a, b, (((1,), (1,)), ((), ())), preferred_element_type=F32)


def t_dot(a, b):
    return lax.dot_general(a, b, (((0,), (0,)), ((), ())), preferred_element_type=F32)


def iota(shape, dim):
    return lax.broadcasted_iota(jnp.int32, shape, dim)


def stats(values):
    center = jnp.sum(values, axis=-1, keepdims=True) * (1.0 / C)
    shifted = values - center
    spread = jnp.sum(shifted * shifted, axis=-1, keepdims=True) * (1.0 / C)
    inverse = lax.rsqrt(spread + EPS)
    return shifted * inverse, inverse


def norm_back(values, grad):
    hat, inverse = stats(values)
    mean_grad = jnp.sum(grad, axis=-1, keepdims=True) * (1.0 / C)
    mean_dot = jnp.sum(grad * hat, axis=-1, keepdims=True) * (1.0 / C)
    return inverse * (grad - mean_grad - hat * mean_dot)


def by_heads(values):
    lane_head = iota(values.shape, 1) // HD
    zero = jnp.zeros_like(values)
    return jnp.concatenate([jnp.where(lane_head == h, values, zero) for h in range(HEADS)], axis=0)


def gather_heads(stacked):
    lane_head = iota((64, C), 1) // HD
    total = jnp.zeros((64, C), F32)
    for h in range(HEADS):
        total = jnp.where(lane_head == h, stacked[h * 64 : h * 64 + 64], total)
    return total


def head_reduce(scores, reduce, fill):
    pieces = []
    for pair in range(3):
        part = scores[:, pair * 128 : pair * 128 + 128]
        first = iota(part.shape, 1) < 64
        low = reduce(jnp.where(first, part, fill), axis=-1, keepdims=True)
        high = reduce(jnp.where(first, fill, part), axis=-1, keepdims=True)
        pieces.append(jnp.where(first, low, high))
    return jnp.concatenate(pieces, axis=1)


def softmax_window(q, k_heads, z_q, z_heads, bias):
    scores = dot_t(q, k_heads) * SCALE + bias
    scores = jnp.where(dot_t(z_q, z_heads) > 0.5, scores, MASKED)
    exponent = jnp.exp(scores - head_reduce(scores, jnp.max, -jnp.inf))
    return exponent / head_reduce(exponent, jnp.sum, 0.0)


def tile_ids(ids):
    z = (iota(ids.shape, 1).astype(F32) == ids).astype(BF16)
    return z, jnp.concatenate([z] * HEADS, axis=0)


def gelu_parts(pre):
    cdf = 0.5 * (1.0 + lax.erf(pre * (1.0 / math.sqrt(2.0))))
    slope = cdf + pre * (jnp.exp(-0.5 * pre * pre) * (1.0 / math.sqrt(2.0 * math.pi)))
    return pre * cdf, slope


def split(values):
    high = values.astype(BF16)
    rest = values - high.astype(F32)
    middle = rest.astype(BF16)
    low = (rest - middle.astype(F32)).astype(BF16)
    return jnp.concatenate([high, middle, low], axis=0)


def joined(pieces):
    n = pieces.shape[0] // 3
    return pieces[0:n] + pieces[n : 2 * n] + pieces[2 * n :]


def offset_onehots(out_ref):
    lane = iota((1, 128), 1)
    row = iota((256, 128), 0)
    for ci in range(WIN):
        offset = jnp.where(lane < 120, (14 - lane // 8) * 15 + (ci - lane % 8 + 7), -1)
        out_ref[ci] = (row == offset).astype(BF16)


def spread_bias(R):
    R.tab[...] = jnp.zeros((16, 256), F32)
    for b in range(2):
        R.tab[b * 8 : b * 8 + 6, 0:225] = R.table[:, b, :]
    pieces = split(R.tab[...])
    per_column = [joined(dot(pieces, R.offsets[ci])) for ci in range(WIN)]
    first = iota((8, 128), 1) < 64
    for b in range(2):
        per_head = [
            jnp.concatenate([per_column[ci][b * 8 + h : b * 8 + h + 1] for ci in range(WIN)], axis=0)
            for h in range(HEADS)
        ]
        for ri in range(WIN):
            shift = (7 - ri) * 8
            for pair in range(3):
                low = pltpu.roll(per_head[2 * pair], (128 - shift) % 128, 1)
                high = pltpu.roll(per_head[2 * pair + 1], (64 - shift) % 128, 1)
                R.bias[b, ri * 8 : ri * 8 + 8, pair * 128 : pair * 128 + 128] = jnp.where(first, low, high)


def fold_bias(grad_ref, offsets):
    first = iota((8, 128), 1) < 64
    per_head = [jnp.zeros((8, 128), F32) for _ in range(HEADS)]
    for ri in range(WIN):
        shift = (7 - ri) * 8
        for pair in range(3):
            part = grad_ref[ri * 8 : ri * 8 + 8, pair * 128 : pair * 128 + 128]
            low = pltpu.roll(jnp.where(first, part, 0.0), shift % 128, 1)
            high = pltpu.roll(jnp.where(first, 0.0, part), (shift + 64) % 128, 1)
            per_head[2 * pair] = per_head[2 * pair] + low
            per_head[2 * pair + 1] = per_head[2 * pair + 1] + high
    total = jnp.zeros((8, 256), F32)
    for ci in range(WIN):
        rows = jnp.concatenate([per_head[h][ci : ci + 1] for h in range(HEADS)] + [jnp.zeros((2, 128), F32)], axis=0)
        total = total + joined(dot_t(split(rows), offsets[ci]))
    return total


def place():
    r = lax.axis_index("rows")
    c = lax.axis_index("cols")
    return r, c


class Net:
    def __init__(self):
        r, c = place()
        self.r, self.c = r, c
        self.x_lo, self.z = r // 8, r % 8
        self.y, self.x_hi, self.core = c // 4, (c // 2) % 2, c % 2
        self.x = self.x_hi * 2 + self.x_lo

    def near(self, dr, dc):
        return ((self.r + dr + 16) % 16, (self.c + dc + 32) % 32)

    def partner(self):
        return (self.r, self.c + 1 - 2 * self.core)

    def at_x(self, x):
        return ((x % 2) * 8 + self.z, self.y * 4 + (x // 2) * 2 + self.core)

    def at_y(self, y):
        return (self.r, y * 4 + self.x_hi * 2 + self.core)

    def at_z(self, z):
        return (self.x_lo * 8 + z, self.c)

    def everyone(self):
        peers = [self.near(dr, dc) for dr, dc in SIDES] + [self.partner()]
        peers += [self.at_x((self.x + d) % 4) for d in range(1, 4)]
        peers += [self.at_y((self.y + d) % 8) for d in range(1, 8)]
        peers += [self.at_z((self.z + d) % 8) for d in range(1, 8)]
        return peers


SIDES = ((-1, 0), (1, 0), (0, -1), (0, 1), (-1, -1), (-1, 1), (1, -1), (1, 1))
SIDE_ROWS = (128, 128, 64, 64, 16, 16, 16, 16)
BACK_ROWS = (128, 128, 32, 32, 16, 16, 16, 16)


def remote(src, dst, send, recv, device):
    return pltpu.make_async_remote_copy(
        src_ref=src, dst_ref=dst, send_sem=send, recv_sem=recv, device_id=device, device_id_type=MESH
    )


def body(*refs):
    R = types.SimpleNamespace(**jax.tree.unflatten(STRUCTURE, refs[COUNT:]))
    R.tokens, R.ids, R.upper, R.upper_ids, R.lower, R.lower_ids, R.cot = refs[:7]
    R.qkv_w, R.proj_w, R.inner_w, R.outer_w, R.table, R.token_grad, R.qkv_grad = refs[7:14]
    R.proj_grad, R.inner_grad, R.outer_grad, R.table_grad = refs[14:COUNT]
    N = Net()

    barrier = pltpu.get_barrier_semaphore()
    peers = N.everyone()
    for peer in peers:
        pl.semaphore_signal(barrier, inc=1, device_id=peer, device_id_type=MESH)

    setup(R)
    forward_one(R)
    pl.semaphore_wait(barrier, len(peers))
    exchange_forward(R, N)
    forward_two(R)
    attend_back_two(R)
    send_back(R, N)
    grads_of(R, N, 1)
    start_core(R, N, 1)
    receive_back(R, N)
    channel_back_one(R)
    start_x(R, N, 1)
    attend_back_one(R)
    start_y(R, N, 1)
    finish_one(R)
    grads_of(R, N, 0)
    start_core(R, N, 0)
    start_z(R, N, 1)
    start_x(R, N, 0)
    finish_z(R, N, 1)
    start_y(R, N, 0)
    start_z(R, N, 0)
    finish_z(R, N, 0)
    finish_table(R)


def select_column(rows, order, ids):
    n = ids.shape[0]
    row_of, col_of = order
    pick = (iota((rows, n), 1) == row_of(iota((rows, n), 0))).astype(BF16)
    spread = dot(pick, ids.astype(F32).astype(BF16))
    keep = iota((rows, 32), 1) == col_of(iota((rows, 32), 0))
    column = jnp.sum(jnp.where(keep, spread, 0.0), axis=-1, keepdims=True)
    return jnp.broadcast_to(column, (rows, 128))


def setup(R):
    offset_onehots(R.offsets)
    spread_bias(R)
    for b in range(2):
        for i, ref in enumerate((R.wq, R.wk, R.wv)):
            ref[b] = R.qkv_w[b][:, i * C : i * C + C]
    for r in range(8):
        row = R.tokens[r].astype(F32)
        for w in range(4):
            R.x1[w * 64 + r * 8 : w * 64 + r * 8 + 8, :] = row[w * 8 : w * 8 + 8]
    by_window = (lambda t: (t // 8) % 8, lambda t: (t // 64) * 8 + t % 8)
    by_row = (lambda t: t // 32, lambda t: t % 32)
    R.id1[...] = select_column(256, by_window, R.ids[...])
    R.rim_id[0] = select_column(128, by_row, R.upper_ids[...])
    R.rim_id[1] = select_column(128, by_row, R.lower_ids[...])
    lane = iota((1, 1024), 1)
    inside = lane % 128
    row = (lane // 128 % 2 * 8 + inside // 12) * 48 + lane // 256 * 12 + inside % 12
    row = jnp.where(inside < 96, row, -1)
    R.pick_hid[...] = (iota((HID, 1024), 0) == row).astype(BF16)
    lane = iota((1, 256), 1)
    inside = lane % 128
    row = jnp.where(inside < 96, lane // 128 * 96 + inside, -1)
    R.pick_ch[...] = (iota((C, 256), 0) == row).astype(BF16)
    out = iota((4 * CHUNK, 1), 0)
    q, k = out // CHUNK, out % CHUNK
    hid = (k - 48) // 6
    col = jnp.where(
        k < 18,
        18 * q + k,
        jnp.where(
            k < 24,
            72 + 6 * q + k - 18,
            jnp.where(k < 48, 96 + 24 * q + k - 24, 192 + 24 * hid + 6 * q + (k - 48 - 6 * hid)),
        ),
    )
    col = jnp.where(k < 72, col, -1)
    R.cut[...] = (iota((4 * CHUNK, 288), 1) == col).astype(BF16)


def forward_one(R):
    @pl.loop(0, 2)
    def _(i):
        at = pl.ds(pl.multiple_of(i * 128, 128), 128)
        normed = stats(R.x1[at, :])[0].astype(BF16)
        R.n1[at, :] = normed
        for ref, weight in ((R.q1, R.wq), (R.k1, R.wk), (R.v1, R.wv)):
            ref[at, :] = dot(normed, weight[0]).astype(BF16)

    @pl.loop(0, 4)
    def _(w):
        at = pl.ds(pl.multiple_of(w * 64, 64), 64)
        z, z_heads = tile_ids(R.id1[at, :])
        probs = softmax_window(R.q1[at, :], by_heads(R.k1[at, :]), z, z_heads, R.bias[0])
        R.p1[at, :] = probs
        R.mix1[at, :] = dot(probs.astype(BF16), by_heads(R.v1[at, :])).astype(BF16)

    @pl.loop(0, 2)
    def _(i):
        at = pl.ds(pl.multiple_of(i * 128, 128), 128)
        middle = (R.x1[at, :] + dot(R.mix1[at, :], R.proj_w[0])).astype(BF16).astype(F32)
        R.mid1[at, :] = middle
        normed = stats(middle)[0].astype(BF16)
        R.m1[at, :] = normed
        act, slope = gelu_parts(dot(normed, R.inner_w[0]))
        act = act.astype(BF16)
        R.act1[at, :] = act
        R.slope1[at, :] = slope
        R.first[at, :] = (middle + dot_t(act, R.outer_w[0])).astype(BF16).astype(F32)


def exchange_forward(R, N):
    ext = R.ext
    for w in range(4):
        for r in range(8):
            t = w * 64 + r * 8
            piece = jnp.concatenate([R.first[t : t + 8, :], R.id1[t : t + 8, 0:64]], axis=1)
            ext[4 + r, 4 + w * 8 : 12 + w * 8, :] = piece
    for i, rim in enumerate((R.upper, R.lower)):
        for r in range(4):
            row = rim[r].astype(F32)
            R.rim[i, r] = jnp.concatenate([row, R.rim_id[i, r * 32 : r * 32 + 32, 0:64]], axis=1)
    for side, top in ((0, 4), (1, 8)):
        for r in range(4):
            R.pack[r * 32 : r * 32 + 32, :] = ext[top + r, 4:36, :]
        R.fs[side][...] = R.pack[0:128, :].astype(BF16)
    for side, left in ((2, 4), (3, 32)):
        for r in range(4):
            R.pack[r * 4 : r * 4 + 4, :] = R.rim[0, r, left - 4 : left, :]
            R.pack[48 + r * 4 : 52 + r * 4, :] = R.rim[1, r, left - 4 : left, :]
        for r in range(8):
            R.pack[16 + r * 4 : 20 + r * 4, :] = ext[4 + r, left : left + 4, :]
        R.fs[side][...] = R.pack[0:64, :].astype(BF16)
    for side, top, left in ((4, 4, 4), (5, 4, 32), (6, 8, 4), (7, 8, 32)):
        for r in range(4):
            R.pack[r * 4 : r * 4 + 4, :] = ext[top + r, left : left + 4, :]
        R.fs[side][...] = R.pack[0:16, :].astype(BF16)
    copies = []
    for side, (dr, dc) in enumerate(SIDES):
        copies.append(
            remote(
                R.fs[side], R.fr[side], R.fsend.at[side], R.frecv.at[side], N.near(dr, dc)
            )
        )
        copies[-1].start()
    for copy in copies:
        copy.wait()
    at_top = N.r == 0
    at_bottom = N.r == 15
    R.pack[...] = R.fr[1][...].astype(F32)
    for r in range(4):
        ext[r, 4:36, :] = jnp.where(at_top, R.rim[0, r], R.pack[r * 32 : r * 32 + 32, :])
    R.pack[...] = R.fr[0][...].astype(F32)
    for r in range(4):
        ext[12 + r, 4:36, :] = jnp.where(at_bottom, R.rim[1, r], R.pack[r * 32 : r * 32 + 32, :])
    for strip, above, below, left in ((3, 7, 5, 0), (2, 6, 4, 36)):
        R.pack[0:64, :] = R.fr[strip][...].astype(F32)
        R.pack[64:80, :] = R.fr[above][...].astype(F32)
        R.pack[80:96, :] = R.fr[below][...].astype(F32)
        for r in range(4):
            own = R.pack[r * 4 : r * 4 + 4, :]
            ext[r, left : left + 4, :] = jnp.where(at_top, own, R.pack[64 + r * 4 : 68 + r * 4, :])
            own = R.pack[48 + r * 4 : 52 + r * 4, :]
            ext[12 + r, left : left + 4, :] = jnp.where(at_bottom, own, R.pack[80 + r * 4 : 84 + r * 4, :])
        for r in range(8):
            ext[4 + r, left : left + 4, :] = R.pack[16 + r * 4 : 20 + r * 4, :]


def query_start(n):
    return n * 64 + (1 - n // 5) * 32


def forward_two(R):
    ext = R.ext
    for a in range(2):
        for b in range(5):
            for i in range(8):
                t = ((a * 5 + b) * 8 + i) * 8
                piece = ext[a * 8 + i, b * 8 : b * 8 + 8, :]
                R.x2[t : t + 8, :] = piece[:, 0:C]
                R.id2[t : t + 8, :] = jnp.broadcast_to(piece[:, C : C + 1], (8, 128))
    R.cot_ext[...] = jnp.zeros_like(R.cot_ext)
    for r in range(8):
        R.cot_ext[r, 4:36, :] = R.cot[r].astype(F32)
    for a in range(2):
        for b in range(5):
            for i in range(4):
                t = (a * 5 + b) * 32 + i * 8
                R.g2[t : t + 8, :] = R.cot_ext[a * 4 + i, b * 8 : b * 8 + 8, :]

    @pl.loop(0, 5)
    def _(i):
        at = pl.ds(pl.multiple_of(i * 128, 128), 128)
        normed = stats(R.x2[at, :])[0].astype(BF16)
        R.n2[at, :] = normed
        for ref, weight in ((R.k2, R.wk), (R.v2, R.wv)):
            ref[at, :] = dot(normed, weight[1]).astype(BF16)

    for n in range(10):
        start = query_start(n)
        R.nq2[n * 32 : n * 32 + 32, :] = R.n2[start : start + 32, :]
        R.xq2[n * 32 : n * 32 + 32, :] = R.x2[start : start + 32, :]
    R.q2[...] = dot(R.nq2[...], R.wq[1]).astype(BF16)

    @pl.loop(0, 10)
    def _(n):
        keys = pl.ds(pl.multiple_of(n * 64, 64), 64)
        queries = pl.ds(pl.multiple_of(n * 32, 32), 32)
        half = pl.ds(pl.multiple_of((1 - n // 5) * 32, 32), 32)
        within = pl.ds(pl.multiple_of(query_start(n), 32), 32)
        z_heads = tile_ids(R.id2[keys, :])[1]
        z = tile_ids(R.id2[within, :])[0]
        probs = softmax_window(R.q2[queries, :], by_heads(R.k2[keys, :]), z, z_heads, R.bias[1, half, :])
        R.p2[queries, :] = probs
        R.mix2[queries, :] = dot(probs.astype(BF16), by_heads(R.v2[keys, :])).astype(BF16)

    @pl.loop(0, 2)
    def _(i):
        at = pl.ds(pl.multiple_of(i * 160, 32), 160)
        middle = (R.xq2[at, :] + dot(R.mix2[at, :], R.proj_w[1])).astype(BF16).astype(F32)
        normed = stats(middle)[0].astype(BF16)
        R.m2[at, :] = normed
        act, slope = gelu_parts(dot(normed, R.inner_w[1]))
        R.act2[at, :] = act.astype(BF16)
        grad_out = R.g2[at, :]
        grad_pre = (slope * dot(grad_out.astype(BF16), R.outer_w[1])).astype(BF16)
        R.pre2[at, :] = grad_pre
        grad_mid = (grad_out + norm_back(middle, dot_t(grad_pre, R.inner_w[1]))).astype(BF16)
        R.gm2[at, :] = grad_mid
        R.e2[at, :] = dot_t(grad_mid, R.proj_w[1]).astype(BF16)


def window_back(probs, e, q, k_heads, v_heads):
    grad_probs = dot_t(e, v_heads)
    grad_scores = probs * (grad_probs - head_reduce(grad_probs * probs, jnp.sum, 0.0))
    low = grad_scores.astype(BF16)
    grad_q = (dot(low, k_heads) * SCALE).astype(BF16)
    grad_k = (gather_heads(t_dot(low, q)) * SCALE).astype(BF16)
    grad_v = gather_heads(t_dot(probs.astype(BF16), e)).astype(BF16)
    return grad_scores, grad_q, grad_k, grad_v


def attend_back_two(R):
    R.gb[1] = jnp.zeros((64, 384), F32)

    @pl.loop(0, 10)
    def _(n):
        keys = pl.ds(pl.multiple_of(n * 64, 64), 64)
        queries = pl.ds(pl.multiple_of(n * 32, 32), 32)
        half = pl.ds(pl.multiple_of((1 - n // 5) * 32, 32), 32)
        grad_scores, grad_q, grad_k, grad_v = window_back(
            R.p2[queries, :],
            R.e2[queries, :],
            R.q2[queries, :],
            by_heads(R.k2[keys, :]),
            by_heads(R.v2[keys, :]),
        )
        R.gb[1, half, :] = R.gb[1, half, :] + grad_scores
        R.dq2[queries, :] = grad_q
        R.dk2[keys, :] = grad_k
        R.dv2[keys, :] = grad_v

    R.dnq2[...] = dot_t(R.dq2[...], R.wq[1])

    @pl.loop(0, 5)
    def _(i):
        at = pl.ds(pl.multiple_of(i * 128, 128), 128)
        R.dn2[at, :] = dot_t(R.dk2[at, :], R.wk[1]) + dot_t(R.dv2[at, :], R.wv[1])

    @pl.loop(0, 10)
    def _(n):
        queries = pl.ds(pl.multiple_of(n * 32, 32), 32)
        within = pl.ds(pl.multiple_of(query_start(n), 32), 32)
        R.dn2[within, :] = R.dn2[within, :] + R.dnq2[queries, :]

    @pl.loop(0, 5)
    def _(i):
        at = pl.ds(pl.multiple_of(i * 128, 128), 128)
        R.dn2[at, :] = norm_back(R.x2[at, :], R.dn2[at, :])

    @pl.loop(0, 10)
    def _(n):
        queries = pl.ds(pl.multiple_of(n * 32, 32), 32)
        within = pl.ds(pl.multiple_of(query_start(n), 32), 32)
        R.dn2[within, :] = R.dn2[within, :] + R.gm2[queries, :].astype(F32)


def back_copy(R, N, side):
    dr, dc = SIDES[side]
    return remote(R.bs[side], R.br[side], R.bsend.at[side], R.brecv.at[side], N.near(dr, dc))


def send_back(R, N):
    ext = R.dext
    for a in range(2):
        for b in range(5):
            for i in range(8):
                t = ((a * 5 + b) * 8 + i) * 8
                ext[a * 8 + i, b * 8 : b * 8 + 8, :] = R.dn2[t : t + 8, :]
    pack = R.pack
    for side, top in ((0, 0), (1, 12)):
        for r in range(4):
            pack[r * 32 : r * 32 + 32, 0:C] = ext[top + r, 4:36, :]
        R.bs[side][...] = pack[0:128, 0:C].astype(BF16)
    for side, left in ((2, 0), (3, 36)):
        for r in range(8):
            pack[r * 4 : r * 4 + 4, 0:C] = ext[4 + r, left : left + 4, :]
        R.bs[side][...] = pack[0:32, 0:C].astype(BF16)
    for side, top, left in ((4, 0, 0), (5, 0, 36), (6, 12, 0), (7, 12, 36)):
        for r in range(4):
            pack[r * 4 : r * 4 + 4, 0:C] = ext[top + r, left : left + 4, :]
        R.bs[side][...] = pack[0:16, 0:C].astype(BF16)
    for side in range(8):
        back_copy(R, N, side).start()


def receive_back(R, N):
    for side in range(8):
        back_copy(R, N, side).wait()
    ext, pack = R.dext, R.pack
    above = jnp.where(N.r == 0, 0.0, 1.0).astype(F32)
    below = jnp.where(N.r == 15, 0.0, 1.0).astype(F32)
    pack[...] = jnp.zeros_like(pack)
    for side, top, left, rows, cols, keep in (
        (1, 4, 4, 4, 32, above),
        (0, 8, 4, 4, 32, below),
        (3, 4, 4, 8, 4, None),
        (2, 4, 32, 8, 4, None),
        (7, 4, 4, 4, 4, above),
        (6, 4, 32, 4, 4, above),
        (5, 8, 4, 4, 4, below),
        (4, 8, 32, 4, 4, below),
    ):
        received = R.br[side][...].astype(F32)
        if keep is not None:
            received = jnp.where(keep > 0.5, received, 0.0)
        pack[0 : BACK_ROWS[side], 0:C] = received
        for r in range(rows):
            ext[top + r, left : left + cols, :] = (
                ext[top + r, left : left + cols, :] + pack[r * cols : r * cols + cols, 0:C]
            )
    for w in range(4):
        for r in range(8):
            t = w * 64 + r * 8
            R.g1[t : t + 8, :] = ext[4 + r, 4 + w * 8 : 12 + w * 8, :]


def channel_back_one(R):
    @pl.loop(0, 2)
    def _(i):
        at = pl.ds(pl.multiple_of(i * 128, 128), 128)
        grad_out = R.g1[at, :].astype(BF16)
        R.gf1[at, :] = grad_out
        grad_pre = (R.slope1[at, :] * dot(grad_out, R.outer_w[0])).astype(BF16)
        R.pre1[at, :] = grad_pre
        back = norm_back(R.mid1[at, :], dot_t(grad_pre, R.inner_w[0]))
        grad_mid = (grad_out.astype(F32) + back).astype(BF16)
        R.gm1[at, :] = grad_mid
        R.e1[at, :] = dot_t(grad_mid, R.proj_w[0]).astype(BF16)


def attend_back_one(R):
    R.gb[0] = jnp.zeros((64, 384), F32)

    @pl.loop(0, 4)
    def _(w):
        at = pl.ds(pl.multiple_of(w * 64, 64), 64)
        grad_scores, grad_q, grad_k, grad_v = window_back(
            R.p1[at, :],
            R.e1[at, :],
            R.q1[at, :],
            by_heads(R.k1[at, :]),
            by_heads(R.v1[at, :]),
        )
        R.gb[0] = R.gb[0] + grad_scores
        R.dq1[at, :] = grad_q
        R.dk1[at, :] = grad_k
        R.dv1[at, :] = grad_v


def finish_one(R):
    @pl.loop(0, 2)
    def _(i):
        at = pl.ds(pl.multiple_of(i * 128, 128), 128)
        grad = dot_t(R.dq1[at, :], R.wq[0])
        grad = grad + dot_t(R.dk1[at, :], R.wk[0]) + dot_t(R.dv1[at, :], R.wv[0])
        R.x1[at, :] = R.gm1[at, :].astype(F32) + norm_back(R.x1[at, :], grad)

    for r in range(8):
        row = [R.x1[w * 64 + r * 8 : w * 64 + r * 8 + 8, :] for w in range(4)]
        R.token_grad[r] = jnp.concatenate(row, axis=0).astype(BF16)


def grads_of(R, N, b):
    pick = R.pick_ch[...]
    normed = dot((R.n1, R.n2)[b][...], pick).astype(BF16)
    query_normed = dot(R.nq2[...], pick).astype(BF16) if b else normed
    R.t_qkv[0:C, :] = t_dot((R.dq1, R.dq2)[b][...], query_normed)
    R.t_qkv[C : 2 * C, :] = t_dot((R.dk1, R.dk2)[b][...], normed)
    R.t_qkv[2 * C : 3 * C, :] = t_dot((R.dv1, R.dv2)[b][...], normed)
    R.t_proj[...] = t_dot((R.gm1, R.gm2)[b][...], dot((R.mix1, R.mix2)[b][...], pick).astype(BF16))
    R.t_inner[...] = t_dot((R.pre1, R.pre2)[b][...], dot((R.m1, R.m2)[b][...], pick).astype(BF16))
    grad_out = R.g2[...].astype(BF16) if b else R.gf1[...]
    for s in range(4):
        act = dot((R.act1, R.act2)[b][...], R.pick_hid[:, s * 256 : s * 256 + 256]).astype(BF16)
        R.t_outer[s] = t_dot(grad_out, act)

    @pl.loop(0, 8)
    def _(y):
        def part(ref, width):
            return ref[pl.ds(pl.multiple_of(y * width, 8), width), :]

        stacked = [part(R.t_qkv, 72), part(R.t_proj, 24), part(R.t_inner, 96)]
        stacked += [part(R.t_outer.at[s], 24) for s in range(4)]
        chunks = dot(R.cut[...], jnp.concatenate(stacked, axis=0).astype(BF16)).astype(BF16)
        for q in range(4):
            for x_lo in range(2):
                R.ga[b, q % 2, q // 2 * 2 + x_lo, y] = chunks[
                    q * CHUNK : q * CHUNK + CHUNK, x_lo * 128 : x_lo * 128 + 128
                ]

    R.tab[b * 8 : b * 8 + 8, :] = fold_bias(R.gb.at[b], R.offsets)


def core_copy(R, N, b):
    return remote(
        R.ga.at[b, 1 - N.core], R.ra.at[b], R.asend.at[b], R.arecv.at[b], N.partner()
    )


def start_core(R, N, b):
    core_copy(R, N, b).start()
    if b == 0:
        R.ta[...] = R.tab[...].astype(BF16)
        table_copy(R, N).start()


def table_copy(R, N):
    return remote(R.ta, R.rta, R.tsend.at[0], R.trecv.at[0], N.partner())


def spread_copies(R, send, recv, src, dst, base, me, n, device):
    def sending(other, d):
        return remote(src(other), dst(me), send.at[base + d], recv.at[base + me], device(other))

    def arriving(other, d):
        return remote(src(other), dst(other), send.at[base + d], recv.at[base + other], device(other))

    return [(functools.partial(sending, (me + d) % n, d), functools.partial(arriving, (me + d) % n, d)) for d in range(1, n)]


def x_copies(R, N, b):
    return spread_copies(
        R, R.xsend, R.xrecv, lambda o: R.hb.at[b, o], lambda s: R.rb.at[b, s], b * 4, N.x, 4, N.at_x
    )


def y_copies(R, N, b):
    return spread_copies(
        R, R.ysend, R.yrecv, lambda o: R.hc.at[b, o], lambda s: R.rc.at[b, s], b * 8, N.y, 8, N.at_y
    )


def z_copies(R, N, b):
    return spread_copies(
        R, R.zsend, R.zrecv, lambda o: R.hd.at[b, o], lambda s: R.rd.at[b, s], b * 8, N.z, 8, N.at_z
    )


def table_copies(R, N, stage):
    me, n, device = ((N.x, 4, N.at_x), (N.y, 8, N.at_y), (N.z, 8, N.at_z))[stage]
    base = stage * 8
    src, dst = R.table_out[stage], R.table_in[stage]
    return spread_copies(
        R, R.tbsend, R.tbrecv, lambda o: src, lambda s: dst.at[s], base, me, n, device
    )


def go(copies):
    for sending, _ in copies:
        sending().start()


def settle(copies):
    for sending, arriving in copies:
        sending().wait_send()
        arriving().wait_recv()


def table_sum(R, N, stage):
    settle(table_copies(R, N, stage))
    n = 8 if stage else 4
    received = R.table_in[stage]
    total = received[0].astype(F32)
    for s in range(1, n):
        total = total + received[s].astype(F32)
    return total


def table_send(R, N, stage, total):
    me = (N.x, N.y, N.z)[stage]
    low = total.astype(BF16)
    R.table_out[stage][...] = low
    R.table_in[stage][me] = low
    go(table_copies(R, N, stage))


def start_x(R, N, b):
    core_copy(R, N, b).wait()

    @pl.loop(0, 4)
    def _(x):
        for y in range(8):
            total = R.ga[b, N.core, x, y].astype(F32) + R.ra[b, x, y].astype(F32)
            R.hb[b, x, y] = total.astype(BF16)

    go(x_copies(R, N, b))
    if b == 0:
        table_copy(R, N).wait()
        table_send(R, N, 0, R.ta[...].astype(F32) + R.rta[...].astype(F32))


def start_y(R, N, b):
    settle(x_copies(R, N, b))

    @pl.loop(0, 8)
    def _(y):
        total = R.hb[b, N.x, y].astype(F32)
        for d in range(1, 4):
            total = total + R.rb[b, (N.x + d) % 4, y].astype(F32)
        R.hc[b, y] = total.astype(BF16)

    go(y_copies(R, N, b))
    if b == 0:
        table_send(R, N, 1, table_sum(R, N, 0))


def start_z(R, N, b):
    settle(y_copies(R, N, b))
    total = R.hc[b, N.y].astype(F32)
    for d in range(1, 8):
        total = total + R.rc[b, (N.y + d) % 8].astype(F32)
    R.turn[...] = jnp.concatenate([total, jnp.zeros((128 - CHUNK, 128), F32)], axis=0).T
    for z in range(8):
        R.hd[b, z] = R.turn[z * 12 : z * 12 + 16, :].astype(BF16)
    go(z_copies(R, N, b))
    if b == 0:
        table_send(R, N, 2, table_sum(R, N, 1))


def finish_z(R, N, b):
    settle(z_copies(R, N, b))
    total = R.hd[b, N.z].astype(F32)
    for d in range(1, 8):
        total = total + R.rd[b, (N.z + d) % 8].astype(F32)
    total = total * (1.0 / 512.0)
    R.qkv_grad[:, b, :] = total[0:12, 0:18]
    R.inner_grad[:, b, :] = total[0:12, 24:48]
    turned = jnp.concatenate([total, jnp.zeros((112, 128), F32)], axis=0).T
    R.proj_grad[:, b, :] = turned[18:24, 0:12]
    outer = [turned[48 + 6 * s : 54 + 6 * s, 0:12] for s in range(4)]
    R.outer_grad[:, b, :] = jnp.concatenate(outer, axis=1)
    if b == 0:
        R.tab[...] = table_sum(R, N, 2) * (1.0 / 512.0)


def finish_table(R):
    for b in range(2):
        R.table_grad[:, b, :] = R.tab[b * 8 : b * 8 + 6, 0:225]


def scratch():
    def f(*shape):
        return pltpu.VMEM(shape, F32)

    def h(*shape):
        return pltpu.VMEM(shape, BF16)

    def semaphores(count):
        return pltpu.SemaphoreType.DMA((count,))

    out = dict(wq=h(2, C, C), wk=h(2, C, C), wv=h(2, C, C), bias=f(2, 64, 384))
    out.update(x1=f(256, C), id1=f(256, 128), rim_id=f(2, 128, 128), rim=f(2, 4, 32, CW))
    out.update(pick_hid=h(HID, 1024), pick_ch=h(C, 256), cut=h(4 * CHUNK, 288))
    out.update(n1=h(256, C), q1=h(256, C), k1=h(256, C), v1=h(256, C), mix1=h(256, C), m1=h(256, C))
    out.update(gf1=h(256, C), gm1=h(256, C), e1=h(256, C), dq1=h(256, C), dk1=h(256, C), dv1=h(256, C))
    out.update(p1=f(256, 384), mid1=f(256, C), first=f(256, C), g1=f(256, C))
    out.update(act1=h(256, HID), slope1=f(256, HID), pre1=h(256, HID))
    out.update(ext=f(16, 40, CW), dext=f(16, 40, C), cot_ext=f(8, 40, C), pack=f(128, CW))
    out.update(x2=f(640, C), id2=f(640, 128), dn2=f(640, C))
    out.update(n2=h(640, C), k2=h(640, C), v2=h(640, C), dk2=h(640, C), dv2=h(640, C))
    out.update(nq2=h(320, C), q2=h(320, C), mix2=h(320, C), m2=h(320, C), gm2=h(320, C), e2=h(320, C), dq2=h(320, C))
    out.update(xq2=f(320, C), g2=f(320, C), dnq2=f(320, C), p2=f(320, 384))
    out.update(act2=h(320, HID), pre2=h(320, HID), gb=f(2, 64, 384))
    out.update(t_qkv=f(576, 256), t_proj=f(C, 256), t_inner=f(HID, 256), t_outer=f(4, C, 256))
    out.update(offsets=h(WIN, 256, 128), tab=f(16, 256), turn=f(128, 128))
    out.update(fs=[h(n, CW) for n in SIDE_ROWS], fr=[h(n, CW) for n in SIDE_ROWS])
    out.update(bs=[h(n, C) for n in BACK_ROWS], br=[h(n, C) for n in BACK_ROWS])
    out.update(ga=h(2, 2, 4, 8, CHUNK, 128), ra=h(2, 4, 8, CHUNK, 128))
    out.update(hb=h(2, 4, 8, CHUNK, 128), rb=h(2, 4, 8, CHUNK, 128))
    out.update(hc=h(2, 8, CHUNK, 128), rc=h(2, 8, CHUNK, 128), hd=h(2, 8, 16, 128), rd=h(2, 8, 16, 128))
    out.update(ta=h(16, 256), rta=h(16, 256), table_out=[h(16, 256)] * 3)
    out.update(table_in=[h(4, 16, 256), h(8, 16, 256), h(8, 16, 256)])
    out.update(fsend=semaphores(8), frecv=semaphores(8), bsend=semaphores(8), brecv=semaphores(8))
    out.update(asend=semaphores(2), arecv=semaphores(2), tsend=semaphores(1), trecv=semaphores(1))
    out.update(xsend=semaphores(8), xrecv=semaphores(8), ysend=semaphores(16), yrecv=semaphores(16))
    out.update(zsend=semaphores(16), zrecv=semaphores(16), tbsend=semaphores(24), tbrecv=semaphores(24))
    return out


SHAPES, STRUCTURE = jax.tree.flatten(scratch(), is_leaf=lambda x: not isinstance(x, (dict, list)))
COUNT = 18


def local(
    tokens,
    region_ids,
    upper_rim,
    upper_ids,
    lower_rim,
    lower_ids,
    cotangent,
    qkv_weight,
    proj_weight,
    inner_weight,
    outer_weight,
    bias_table,
):
    out = pl.pallas_call(
        body,
        out_shape=(
            jax.ShapeDtypeStruct((8, 32, C), BF16),
            jax.ShapeDtypeStruct((12, 2, 18), F32),
            jax.ShapeDtypeStruct((6, 2, 12), F32),
            jax.ShapeDtypeStruct((12, 2, 24), F32),
            jax.ShapeDtypeStruct((6, 2, 48), F32),
            jax.ShapeDtypeStruct((6, 2, 225), F32),
        ),
        in_specs=[pl.BlockSpec(memory_space=pltpu.VMEM)] * 12,
        out_specs=[pl.BlockSpec(memory_space=pltpu.VMEM)] * 6,
        scratch_shapes=SHAPES,
        compiler_params=pltpu.CompilerParams(
            collective_id=0, has_side_effects=True, vmem_limit_bytes=60 * 1024 * 1024
        ),
        name="blocks",
    )(
        tokens,
        region_ids,
        upper_rim,
        upper_ids,
        lower_rim,
        lower_ids,
        cotangent,
        qkv_weight,
        proj_weight,
        inner_weight,
        outer_weight.transpose(0, 2, 1),
        bias_table.transpose(2, 0, 1),
    )
    orders = ((1, 0, 2), (1, 2, 0), (1, 0, 2), (1, 2, 0), (1, 2, 0))
    return (out[0], *(part.transpose(order) for part, order in zip(out[1:], orders)))


def solution(mesh):
    return jax.shard_map(
        local,
        mesh=mesh,
        in_specs=(
            P("rows", "cols", None),
            P("rows", "cols"),
            P(None, "cols", None),
            P(None, "cols"),
            P(None, "cols", None),
            P(None, "cols"),
            P("rows", "cols", None),
            P(),
            P(),
            P(),
            P(),
            P(),
        ),
        out_specs=(
            P("rows", "cols", None),
            P(None, "rows", "cols"),
            P(None, "rows", "cols"),
            P(None, "rows", "cols"),
            P(None, "rows", "cols"),
            P(),
        ),
        check_vma=False,
    )
```

time: 751 us -> 97.3 us (0.13)
  the two profiles are of different devices: /device:TPU:4 before, /device:TPU:1 now
where the time goes in v1:
time: 97.3 us; the launch traced here: 97 us
  Pallas kernels  91.3 us (94%)
  local copies, waits for them, and re-layouts  4.99 us (5%)
    pallas_call x1, Pallas kernels, local(): pl.pallas_call(body, out_shape=(jax.ShapeDtypeStruct((8, 32, C), BF16), j...  91.3 us
    unnamed x16, local copies, waits for them, and re-layouts  4.99 us

profile of v1, /device:TPU:1, one launch (start us, length us, event | category | flops | bytes accessed | tf_op | source)
XLA Modules:
  0.0 97.0 jit_solution(13188232630746745704)
XLA Ops:
  0.6 91.3 %blocks.1 = (bf16[8,32,192]{2,1,0:T(8,128)(2,1)}, f32[12,2,18]{2,1,0:T(2,128)}, f32[6,2,12]{2,1,0:T(2,128)}, f32[12,2,24]{2,1,0:T(2,128)}, f32[6,2,48]{2,1,0:T(2,128)}, /*index=5*/f32[6,2,225]{2,1,0:T(2,128)}) custom-call(bf16[8,32,192]{2,1,0:T(8,128)(2,1)} %refs_0_.1, s32[8,32]{1,0:T(8,128)} %refs_1_.1, bf16[4,32,192]{2,1,0:T(8,128)(2,1)} %refs_2_.1, ...), custom_call_target="tpu_custom_call" | custom-call | tf_op jit(solution)/shard_map/blocks/pallas_call | solution.py:845
  92.0 0.0 copy-start.2
  92.0 1.6 %copy.24 = bf16[8,32,192]{2,1,0:T(8,128)(2,1)} copy(bf16[8,32,192]{2,1,0:T(8,128)(2,1)} %get-tuple-element.24) | data formatting | bytes 196608
  93.6 0.0 copy-done.2
  93.6 0.0 copy-start.4
  93.6 0.6 copy.25
  94.2 0.1 copy-done.4
  94.3 0.0 copy-start.1
  94.3 0.6 copy.26
  94.9 0.1 copy-done.1
  95.0 0.0 copy-start.3
  95.0 0.6 copy.27
  95.6 0.1 copy-done.3
  95.7 0.0 copy-start
  95.7 0.6 copy.28
  96.3 0.1 copy-done
  96.4 0.6 copy.29
Async XLA Ops:
  92.0 1.6 %copy-start.2 = (f32[12,2,18]{2,1,0:T(2,128)S(1)}, f32[12,2,18]{2,1,0:T(2,128)}, u32[]{:S(2)}) copy-start(f32[12,2,18]{2,1,0:T(2,128)} %get-tuple-element.13) | copy-start | bytes 5188
  93.6 0.7 copy-start.4
  94.3 0.7 copy-start.1
  95.0 0.7 copy-start.3
  95.7 0.7 copy-start

commit v2 on v1

--- a/solution.py
+++ b/solution.py
@@ -209,8 +209,8 @@
 def body(*refs):
     R = types.SimpleNamespace(**jax.tree.unflatten(STRUCTURE, refs[COUNT:]))
     R.tokens, R.ids, R.upper, R.upper_ids, R.lower, R.lower_ids, R.cot = refs[:7]
-    R.qkv_w, R.proj_w, R.inner_w, R.outer_w, R.table, R.token_grad, R.qkv_grad = refs[7:14]
-    R.proj_grad, R.inner_grad, R.outer_grad, R.table_grad = refs[14:COUNT]
+    R.qkv_w, R.proj_w, R.inner_w, R.outer_w, R.table, R.token_grad, R.totals = refs[7:14]
+    R.table_total = refs[14]
     N = Net()
 
     barrier = pltpu.get_barrier_semaphore()
@@ -225,23 +225,25 @@
     forward_two(R)
     attend_back_two(R)
     send_back(R, N)
-    grads_of(R, N, 1)
+    grads_of(R, 1)
     start_core(R, N, 1)
+    table_of(R, 1)
     receive_back(R, N)
     channel_back_one(R)
     start_x(R, N, 1)
     attend_back_one(R)
     start_y(R, N, 1)
+    grads_of(R, 0)
+    start_core(R, N, 0)
+    table_of(R, 0)
+    start_table(R, N)
     finish_one(R)
-    grads_of(R, N, 0)
-    start_core(R, N, 0)
     start_z(R, N, 1)
     start_x(R, N, 0)
     finish_z(R, N, 1)
     start_y(R, N, 0)
     start_z(R, N, 0)
     finish_z(R, N, 0)
-    finish_table(R)
 
 
 def select_column(rows, order, ids):
@@ -257,9 +259,8 @@
 def setup(R):
     offset_onehots(R.offsets)
     spread_bias(R)
-    for b in range(2):
-        for i, ref in enumerate((R.wq, R.wk, R.wv)):
-            ref[b] = R.qkv_w[b][:, i * C : i * C + C]
+    for i, ref in enumerate((R.wq, R.wk, R.wv)):
+        ref[0] = R.qkv_w[0][:, i * C : i * C + C]
     for r in range(8):
         row = R.tokens[r].astype(F32)
         for w in range(4):
@@ -269,6 +270,19 @@
     R.id1[...] = select_column(256, by_window, R.ids[...])
     R.rim_id[0] = select_column(128, by_row, R.upper_ids[...])
     R.rim_id[1] = select_column(128, by_row, R.lower_ids[...])
+
+
+def setup_later(R):
+    for i, ref in enumerate((R.wq, R.wk, R.wv)):
+        ref[1] = R.qkv_w[1][:, i * C : i * C + C]
+    R.cot_ext[...] = jnp.zeros_like(R.cot_ext)
+    for r in range(8):
+        R.cot_ext[r, 4:36, :] = R.cot[r].astype(F32)
+    for a in range(2):
+        for b in range(5):
+            for i in range(4):
+                t = (a * 5 + b) * 32 + i * 8
+                R.g2[t : t + 8, :] = R.cot_ext[a * 4 + i, b * 8 : b * 8 + 8, :]
     lane = iota((1, 1024), 1)
     inside = lane % 128
     row = (lane // 128 % 2 * 8 + inside // 12) * 48 + lane // 256 * 12 + inside % 12
@@ -303,13 +317,18 @@
         for ref, weight in ((R.q1, R.wq), (R.k1, R.wk), (R.v1, R.wv)):
             ref[at, :] = dot(normed, weight[0]).astype(BF16)
 
-    @pl.loop(0, 4)
-    def _(w):
-        at = pl.ds(pl.multiple_of(w * 64, 64), 64)
-        z, z_heads = tile_ids(R.id1[at, :])
-        probs = softmax_window(R.q1[at, :], by_heads(R.k1[at, :]), z, z_heads, R.bias[0])
-        R.p1[at, :] = probs
-        R.mix1[at, :] = dot(probs.astype(BF16), by_heads(R.v1[at, :])).astype(BF16)
+    @pl.loop(0, 2)
+    def _(pair):
+        done = []
+        for w in (pair * 2, pair * 2 + 1):
+            at = pl.ds(pl.multiple_of(w * 64, 64), 64)
+            z, z_heads = tile_ids(R.id1[at, :])
+            probs = softmax_window(R.q1[at, :], by_heads(R.k1[at, :]), z, z_heads, R.bias[0])
+            mix = dot(probs.astype(BF16), by_heads(R.v1[at, :])).astype(BF16)
+            done.append((at, probs, mix))
+        for at, probs, mix in done:
+            R.p1[at, :] = probs
+            R.mix1[at, :] = mix
 
     @pl.loop(0, 2)
     def _(i):
@@ -359,6 +378,7 @@
             )
         )
         copies[-1].start()
+    setup_later(R)
     for copy in copies:
         copy.wait()
     at_top = N.r == 0
@@ -395,15 +415,6 @@
                 piece = ext[a * 8 + i, b * 8 : b * 8 + 8, :]
                 R.x2[t : t + 8, :] = piece[:, 0:C]
                 R.id2[t : t + 8, :] = jnp.broadcast_to(piece[:, C : C + 1], (8, 128))
-    R.cot_ext[...] = jnp.zeros_like(R.cot_ext)
-    for r in range(8):
-        R.cot_ext[r, 4:36, :] = R.cot[r].astype(F32)
-    for a in range(2):
-        for b in range(5):
-            for i in range(4):
-                t = (a * 5 + b) * 32 + i * 8
-                R.g2[t : t + 8, :] = R.cot_ext[a * 4 + i, b * 8 : b * 8 + 8, :]
-
     @pl.loop(0, 5)
     def _(i):
         at = pl.ds(pl.multiple_of(i * 128, 128), 128)
@@ -418,17 +429,22 @@
         R.xq2[n * 32 : n * 32 + 32, :] = R.x2[start : start + 32, :]
     R.q2[...] = dot(R.nq2[...], R.wq[1]).astype(BF16)
 
-    @pl.loop(0, 10)
-    def _(n):
-        keys = pl.ds(pl.multiple_of(n * 64, 64), 64)
-        queries = pl.ds(pl.multiple_of(n * 32, 32), 32)
-        half = pl.ds(pl.multiple_of((1 - n // 5) * 32, 32), 32)
-        within = pl.ds(pl.multiple_of(query_start(n), 32), 32)
-        z_heads = tile_ids(R.id2[keys, :])[1]
-        z = tile_ids(R.id2[within, :])[0]
-        probs = softmax_window(R.q2[queries, :], by_heads(R.k2[keys, :]), z, z_heads, R.bias[1, half, :])
-        R.p2[queries, :] = probs
-        R.mix2[queries, :] = dot(probs.astype(BF16), by_heads(R.v2[keys, :])).astype(BF16)
+    @pl.loop(0, 5)
+    def _(b):
+        done = []
+        for n, first in ((b, 32), (b + 5, 0)):
+            keys = pl.ds(pl.multiple_of(n * 64, 64), 64)
+            queries = pl.ds(pl.multiple_of(n * 32, 32), 32)
+            within = pl.ds(pl.multiple_of(n * 64 + first, 32), 32)
+            z_heads = tile_ids(R.id2[keys, :])[1]
+            z = tile_ids(R.id2[within, :])[0]
+            bias = R.bias[1, first : first + 32, :]
+            probs = softmax_window(R.q2[queries, :], by_heads(R.k2[keys, :]), z, z_heads, bias)
+            mix = dot(probs.astype(BF16), by_heads(R.v2[keys, :])).astype(BF16)
+            done.append((queries, probs, mix))
+        for queries, probs, mix in done:
+            R.p2[queries, :] = probs
+            R.mix2[queries, :] = mix
 
     @pl.loop(0, 2)
     def _(i):
@@ -459,22 +475,25 @@
 def attend_back_two(R):
     R.gb[1] = jnp.zeros((64, 384), F32)
 
-    @pl.loop(0, 10)
-    def _(n):
-        keys = pl.ds(pl.multiple_of(n * 64, 64), 64)
-        queries = pl.ds(pl.multiple_of(n * 32, 32), 32)
-        half = pl.ds(pl.multiple_of((1 - n // 5) * 32, 32), 32)
-        grad_scores, grad_q, grad_k, grad_v = window_back(
-            R.p2[queries, :],
-            R.e2[queries, :],
-            R.q2[queries, :],
-            by_heads(R.k2[keys, :]),
-            by_heads(R.v2[keys, :]),
-        )
-        R.gb[1, half, :] = R.gb[1, half, :] + grad_scores
-        R.dq2[queries, :] = grad_q
-        R.dk2[keys, :] = grad_k
-        R.dv2[keys, :] = grad_v
+    @pl.loop(0, 5)
+    def _(b):
+        done = []
+        for n in (b, b + 5):
+            keys = pl.ds(pl.multiple_of(n * 64, 64), 64)
+            queries = pl.ds(pl.multiple_of(n * 32, 32), 32)
+            back = window_back(
+                R.p2[queries, :],
+                R.e2[queries, :],
+                R.q2[queries, :],
+                by_heads(R.k2[keys, :]),
+                by_heads(R.v2[keys, :]),
+            )
+            done.append((keys, queries, back))
+        for half, (keys, queries, back) in zip((32, 0), done):
+            R.gb[1, half : half + 32, :] = R.gb[1, half : half + 32, :] + back[0]
+            R.dq2[queries, :] = back[1]
+            R.dk2[keys, :] = back[2]
+            R.dv2[keys, :] = back[3]
 
     R.dnq2[...] = dot_t(R.dq2[...], R.wq[1])
 
@@ -578,20 +597,20 @@
 def attend_back_one(R):
     R.gb[0] = jnp.zeros((64, 384), F32)
 
-    @pl.loop(0, 4)
-    def _(w):
-        at = pl.ds(pl.multiple_of(w * 64, 64), 64)
-        grad_scores, grad_q, grad_k, grad_v = window_back(
-            R.p1[at, :],
-            R.e1[at, :],
-            R.q1[at, :],
-            by_heads(R.k1[at, :]),
-            by_heads(R.v1[at, :]),
-        )
-        R.gb[0] = R.gb[0] + grad_scores
-        R.dq1[at, :] = grad_q
-        R.dk1[at, :] = grad_k
-        R.dv1[at, :] = grad_v
+    @pl.loop(0, 2)
+    def _(pair):
+        done = []
+        for w in (pair * 2, pair * 2 + 1):
+            at = pl.ds(pl.multiple_of(w * 64, 64), 64)
+            back = window_back(
+                R.p1[at, :], R.e1[at, :], R.q1[at, :], by_heads(R.k1[at, :]), by_heads(R.v1[at, :])
+            )
+            done.append((at, back))
+        for at, back in done:
+            R.gb[0] = R.gb[0] + back[0]
+            R.dq1[at, :] = back[1]
+            R.dk1[at, :] = back[2]
+            R.dv1[at, :] = back[3]
 
 
 def finish_one(R):
@@ -607,7 +626,7 @@
         R.token_grad[r] = jnp.concatenate(row, axis=0).astype(BF16)
 
 
-def grads_of(R, N, b):
+def grads_of(R, b):
     pick = R.pick_ch[...]
     normed = dot((R.n1, R.n2)[b][...], pick).astype(BF16)
     query_normed = dot(R.nq2[...], pick).astype(BF16) if b else normed
@@ -635,6 +654,8 @@
                     q * CHUNK : q * CHUNK + CHUNK, x_lo * 128 : x_lo * 128 + 128
                 ]
 
+
+def table_of(R, b):
     R.tab[b * 8 : b * 8 + 8, :] = fold_bias(R.gb.at[b], R.offsets)
 
 
@@ -646,9 +667,11 @@
 
 def start_core(R, N, b):
     core_copy(R, N, b).start()
-    if b == 0:
-        R.ta[...] = R.tab[...].astype(BF16)
-        table_copy(R, N).start()
+
+
+def start_table(R, N):
+    R.ta[...] = R.tab[...].astype(BF16)
+    table_copy(R, N).start()
 
 
 def table_copy(R, N):
@@ -769,20 +792,22 @@
     total = R.hd[b, N.z].astype(F32)
     for d in range(1, 8):
         total = total + R.rd[b, (N.z + d) % 8].astype(F32)
-    total = total * (1.0 / 512.0)
-    R.qkv_grad[:, b, :] = total[0:12, 0:18]
-    R.inner_grad[:, b, :] = total[0:12, 24:48]
-    turned = jnp.concatenate([total, jnp.zeros((112, 128), F32)], axis=0).T
-    R.proj_grad[:, b, :] = turned[18:24, 0:12]
-    outer = [turned[48 + 6 * s : 54 + 6 * s, 0:12] for s in range(4)]
-    R.outer_grad[:, b, :] = jnp.concatenate(outer, axis=1)
+    R.totals[b] = total
     if b == 0:
-        R.tab[...] = table_sum(R, N, 2) * (1.0 / 512.0)
-
-
-def finish_table(R):
+        R.table_total[...] = table_sum(R, N, 2)
+
+
+def hand_on(summed, totals, table, tokens, qkv, proj, inner, outer, table_grad):
+    tokens[...] = summed[...]
     for b in range(2):
-        R.table_grad[:, b, :] = R.tab[b * 8 : b * 8 + 6, 0:225]
+        total = totals[b] * (1.0 / 512.0)
+        qkv[:, b, :] = total[0:12, 0:18]
+        inner[:, b, :] = total[0:12, 24:48]
+        turned = jnp.concatenate([total, jnp.zeros((112, 128), F32)], axis=0).T
+        proj[:, b, :] = turned[18:24, 0:12]
+        parts = [turned[48 + 6 * s : 54 + 6 * s, 0:12] for s in range(4)]
+        outer[:, b, :] = jnp.concatenate(parts, axis=1)
+        table_grad[:, b, :] = table[b * 8 : b * 8 + 6, 0:225] * (1.0 / 512.0)
 
 
 def scratch():
@@ -825,7 +850,7 @@
 
 
 SHAPES, STRUCTURE = jax.tree.flatten(scratch(), is_leaf=lambda x: not isinstance(x, (dict, list)))
-COUNT = 18
+COUNT = 15
 
 
 def local(
@@ -846,14 +871,11 @@
         body,
         out_shape=(
             jax.ShapeDtypeStruct((8, 32, C), BF16),
-            jax.ShapeDtypeStruct((12, 2, 18), F32),
-            jax.ShapeDtypeStruct((6, 2, 12), F32),
-            jax.ShapeDtypeStruct((12, 2, 24), F32),
-            jax.ShapeDtypeStruct((6, 2, 48), F32),
-            jax.ShapeDtypeStruct((6, 2, 225), F32),
+            jax.ShapeDtypeStruct((2, 16, 128), F32),
+            jax.ShapeDtypeStruct((16, 256), F32),
         ),
         in_specs=[pl.BlockSpec(memory_space=pltpu.VMEM)] * 12,
-        out_specs=[pl.BlockSpec(memory_space=pltpu.VMEM)] * 6,
+        out_specs=[pl.BlockSpec(memory_space=pltpu.VMEM)] * 3,
         scratch_shapes=SHAPES,
         compiler_params=pltpu.CompilerParams(
             collective_id=0, has_side_effects=True, vmem_limit_bytes=60 * 1024 * 1024
@@ -873,6 +895,20 @@
         outer_weight.transpose(0, 2, 1),
         bias_table.transpose(2, 0, 1),
     )
+    out = pl.pallas_call(
+        hand_on,
+        out_shape=(
+            jax.ShapeDtypeStruct((8, 32, C), BF16),
+            jax.ShapeDtypeStruct((12, 2, 18), F32),
+            jax.ShapeDtypeStruct((6, 2, 12), F32),
+            jax.ShapeDtypeStruct((12, 2, 24), F32),
+            jax.ShapeDtypeStruct((6, 2, 48), F32),
+            jax.ShapeDtypeStruct((6, 2, 225), F32),
+        ),
+        in_specs=[pl.BlockSpec(memory_space=pltpu.VMEM)] * 3,
+        out_specs=[pl.BlockSpec(memory_space=pltpu.VMEM)] * 6,
+        name="hand_on",
+    )(*out)
     orders = ((1, 0, 2), (1, 2, 0), (1, 0, 2), (1, 2, 0), (1, 2, 0))
     return (out[0], *(part.transpose(order) for part, order in zip(out[1:], orders)))
 

time: 97.3 us -> 88.9 us (0.914); the launches traced: 97 us -> 87.4 us
  local copies, waits for them, and re-layouts: 4.99 us -> 0 us
  Pallas kernels: 91.3 us -> 86.8 us
    pallas_call x1, Pallas kernels: 91.3 us -> 85.1 us  [local(): pl.pallas_call(body, out_shape=(jax.ShapeDtypeStruct((8, 32, C), BF16), j...]
    unnamed x16 -> x0, local copies, waits for them, and re-layouts: 4.99 us -> none
    pallas_call x0 -> x1, Pallas kernels: none -> 1.7 us  [local(): pl.pallas_call(hand_on, out_shape=(jax.ShapeDtypeStruct((8, 32, C), BF16)...]
where the time goes in v2:
time: 88.9 us; the launch traced here: 87.4 us
  Pallas kernels  86.8 us (98%)
    pallas_call x1, Pallas kernels, local(): pl.pallas_call(body, out_shape=(jax.ShapeDtypeStruct((8, 32, C), BF16), j...  85.1 us

profile of v2, /device:TPU:1, one launch (start us, length us, event | category | flops | bytes accessed | tf_op | source)
XLA Modules:
  0.0 87.4 jit_solution(16416406474559168668)
XLA Ops:
  0.6 85.1 %blocks.1 = (bf16[8,32,192]{2,1,0:T(8,128)(2,1)}, f32[2,16,128]{2,1,0:T(8,128)}, f32[16,256]{1,0:T(8,128)}) custom-call(bf16[8,32,192]{2,1,0:T(8,128)(2,1)} %refs_0_.1, s32[8,32]{1,0:T(8,128)} %refs_1_.1, bf16[4,32,192]{2,1,0:T(8,128)(2,1)} %refs_2_.1, s32[4,32]{1,0:T(4,128)} %refs_3_.1, bf16[4,32,192]{2,1,0:T(8,128)(2,1)} %refs_4_.1, s32[4,32]{1,0:T(4,128)} %refs_5_.1, ...), custom_call_target="tpu_custom_call" | custom-call | tf_op jit(solution)/shard_map/blocks/pallas_call | solution.py:870
  85.7 1.7 %hand_on.1 = (bf16[8,32,192]{2,1,0:T(8,128)(2,1)}, f32[12,2,18]{2,1,0:T(2,128)}, f32[6,2,12]{2,1,0:T(2,128)}, f32[12,2,24]{2,1,0:T(2,128)}, f32[6,2,48]{2,1,0:T(2,128)}, /*index=5*/f32[6,2,225]{2,1,0:T(2,128)}) custom-call(bf16[8,32,192]{2,1,0:T(8,128)(2,1)} %get-tuple-element.15.summed, f32[2,16,128]{2,1,0:T(8,128)} %get-tuple-element.16.totals, ...), custom_call_target="tpu_custom_call" | custom-call | tf_op jit(solution)/shard_map/hand_on/pallas_call | solution.py:898

commit v3 on v2

--- a/solution.py
+++ b/solution.py
@@ -20,6 +20,7 @@
 SCALE = HD**-0.5
 CW = 256
 CHUNK = 80
+TOP = 48
 F32 = jnp.float32
 BF16 = jnp.bfloat16
 MESH = pl.DeviceIdType.MESH
@@ -689,14 +690,28 @@
 
 
 def x_copies(R, N, b):
-    return spread_copies(
-        R, R.xsend, R.xrecv, lambda o: R.hb.at[b, o], lambda s: R.rb.at[b, s], b * 4, N.x, 4, N.at_x
-    )
+    def source(other):
+        return R.hb.at[b, other, :, 0:TOP, :]
+
+    return spread_copies(R, R.xsend, R.xrecv, source, lambda s: R.rb.at[b, s], b * 4, N.x, 4, N.at_x)
 
 
 def y_copies(R, N, b):
     return spread_copies(
         R, R.ysend, R.yrecv, lambda o: R.hc.at[b, o], lambda s: R.rc.at[b, s], b * 8, N.y, 8, N.at_y
+    )
+
+
+def y_first_copies(R, N, b):
+    def source(other):
+        return R.hb.at[b, :, other, TOP:CHUNK, :]
+
+    return spread_copies(R, R.vsend, R.vrecv, source, lambda s: R.rv.at[b, s], b * 8, N.y, 8, N.at_y)
+
+
+def x_second_copies(R, N, b):
+    return spread_copies(
+        R, R.wsend, R.wrecv, lambda o: R.hw.at[b, o], lambda s: R.rw.at[b, s], b * 4, N.x, 4, N.at_x
     )
 
 
@@ -747,13 +762,15 @@
 def start_x(R, N, b):
     core_copy(R, N, b).wait()
 
-    @pl.loop(0, 4)
-    def _(x):
+    over_x = x_copies(R, N, b)
+    for d in (1, 3, 2, 0):
+        x = (N.x + d) % 4
         for y in range(8):
             total = R.ga[b, N.core, x, y].astype(F32) + R.ra[b, x, y].astype(F32)
             R.hb[b, x, y] = total.astype(BF16)
-
-    go(x_copies(R, N, b))
+        if d:
+            go(over_x[d - 1 : d])
+    go(y_first_copies(R, N, b))
     if b == 0:
         table_copy(R, N).wait()
         table_send(R, N, 0, R.ta[...].astype(F32) + R.rta[...].astype(F32))
@@ -764,12 +781,19 @@
 
     @pl.loop(0, 8)
     def _(y):
-        total = R.hb[b, N.x, y].astype(F32)
+        total = R.hb[b, N.x, y, 0:TOP, :].astype(F32)
         for d in range(1, 4):
             total = total + R.rb[b, (N.x + d) % 4, y].astype(F32)
         R.hc[b, y] = total.astype(BF16)
 
     go(y_copies(R, N, b))
+    settle(y_first_copies(R, N, b))
+    for x in range(4):
+        total = R.hb[b, x, N.y, TOP:CHUNK, :].astype(F32)
+        for d in range(1, 8):
+            total = total + R.rv[b, (N.y + d) % 8, x].astype(F32)
+        R.hw[b, x] = total.astype(BF16)
+    go(x_second_copies(R, N, b))
     if b == 0:
         table_send(R, N, 1, table_sum(R, N, 0))
 
@@ -779,7 +803,11 @@
     total = R.hc[b, N.y].astype(F32)
     for d in range(1, 8):
         total = total + R.rc[b, (N.y + d) % 8].astype(F32)
-    R.turn[...] = jnp.concatenate([total, jnp.zeros((128 - CHUNK, 128), F32)], axis=0).T
+    settle(x_second_copies(R, N, b))
+    rest = R.hw[b, N.x].astype(F32)
+    for d in range(1, 4):
+        rest = rest + R.rw[b, (N.x + d) % 4].astype(F32)
+    R.turn[...] = jnp.concatenate([total, rest, jnp.zeros((128 - CHUNK, 128), F32)], axis=0).T
     for z in range(8):
         R.hd[b, z] = R.turn[z * 12 : z * 12 + 16, :].astype(BF16)
     go(z_copies(R, N, b))
@@ -838,14 +866,16 @@
     out.update(fs=[h(n, CW) for n in SIDE_ROWS], fr=[h(n, CW) for n in SIDE_ROWS])
     out.update(bs=[h(n, C) for n in BACK_ROWS], br=[h(n, C) for n in BACK_ROWS])
     out.update(ga=h(2, 2, 4, 8, CHUNK, 128), ra=h(2, 4, 8, CHUNK, 128))
-    out.update(hb=h(2, 4, 8, CHUNK, 128), rb=h(2, 4, 8, CHUNK, 128))
-    out.update(hc=h(2, 8, CHUNK, 128), rc=h(2, 8, CHUNK, 128), hd=h(2, 8, 16, 128), rd=h(2, 8, 16, 128))
+    out.update(hb=h(2, 4, 8, CHUNK, 128), rb=h(2, 4, 8, TOP, 128))
+    out.update(rv=h(2, 8, 4, CHUNK - TOP, 128), hw=h(2, 4, CHUNK - TOP, 128), rw=h(2, 4, CHUNK - TOP, 128))
+    out.update(hc=h(2, 8, TOP, 128), rc=h(2, 8, TOP, 128), hd=h(2, 8, 16, 128), rd=h(2, 8, 16, 128))
     out.update(ta=h(16, 256), rta=h(16, 256), table_out=[h(16, 256)] * 3)
     out.update(table_in=[h(4, 16, 256), h(8, 16, 256), h(8, 16, 256)])
     out.update(fsend=semaphores(8), frecv=semaphores(8), bsend=semaphores(8), brecv=semaphores(8))
     out.update(asend=semaphores(2), arecv=semaphores(2), tsend=semaphores(1), trecv=semaphores(1))
     out.update(xsend=semaphores(8), xrecv=semaphores(8), ysend=semaphores(16), yrecv=semaphores(16))
     out.update(zsend=semaphores(16), zrecv=semaphores(16), tbsend=semaphores(24), tbrecv=semaphores(24))
+    out.update(vsend=semaphores(16), vrecv=semaphores(16), wsend=semaphores(8), wrecv=semaphores(8))
     return out
 
 

time: 88.9 us -> 86.7 us (0.975); the launches traced: 87.4 us -> 86.2 us
  Pallas kernels: 86.8 us -> 85.5 us
    pallas_call x1, Pallas kernels: 85.1 us -> 83.8 us  [local(): pl.pallas_call(body, out_shape=(jax.ShapeDtypeStruct((8, 32, C), BF16), j...]
where the time goes in v3:
time: 86.7 us; the launch traced here: 86.2 us
  Pallas kernels  85.5 us (99%)
    pallas_call x1, Pallas kernels, local(): pl.pallas_call(body, out_shape=(jax.ShapeDtypeStruct((8, 32, C), BF16), j...  83.8 us

profile of v3, /device:TPU:1, one launch (start us, length us, event | category | flops | bytes accessed | tf_op | source)
XLA Modules:
  0.0 86.2 jit_solution(11345088367544833294)
XLA Ops:
  0.6 83.8 %blocks.1 = (bf16[8,32,192]{2,1,0:T(8,128)(2,1)}, f32[2,16,128]{2,1,0:T(8,128)}, f32[16,256]{1,0:T(8,128)}) custom-call(bf16[8,32,192]{2,1,0:T(8,128)(2,1)} %refs_0_.1, s32[8,32]{1,0:T(8,128)} %refs_1_.1, bf16[4,32,192]{2,1,0:T(8,128)(2,1)} %refs_2_.1, s32[4,32]{1,0:T(4,128)} %refs_3_.1, bf16[4,32,192]{2,1,0:T(8,128)(2,1)} %refs_4_.1, s32[4,32]{1,0:T(4,128)} %refs_5_.1, ...), custom_call_target="tpu_custom_call" | custom-call | tf_op jit(solution)/shard_map/blocks/pallas_call | solution.py:900
  84.5 1.7 %hand_on.1 = (bf16[8,32,192]{2,1,0:T(8,128)(2,1)}, f32[12,2,18]{2,1,0:T(2,128)}, f32[6,2,12]{2,1,0:T(2,128)}, f32[12,2,24]{2,1,0:T(2,128)}, f32[6,2,48]{2,1,0:T(2,128)}, /*index=5*/f32[6,2,225]{2,1,0:T(2,128)}) custom-call(bf16[8,32,192]{2,1,0:T(8,128)(2,1)} %get-tuple-element.15.summed, f32[2,16,128]{2,1,0:T(8,128)} %get-tuple-element.16.totals, ...), custom_call_target="tpu_custom_call" | custom-call | tf_op jit(solution)/shard_map/hand_on/pallas_call | solution.py:928

commit v4 on v3

--- a/solution.py
+++ b/solution.py
@@ -226,16 +226,14 @@
     forward_two(R)
     attend_back_two(R)
     send_back(R, N)
-    grads_of(R, 1)
-    start_core(R, N, 1)
+    grads_of(R, N, 1)
     table_of(R, 1)
     receive_back(R, N)
     channel_back_one(R)
     start_x(R, N, 1)
     attend_back_one(R)
     start_y(R, N, 1)
-    grads_of(R, 0)
-    start_core(R, N, 0)
+    grads_of(R, N, 0)
     table_of(R, 0)
     start_table(R, N)
     finish_one(R)
@@ -627,7 +625,7 @@
         R.token_grad[r] = jnp.concatenate(row, axis=0).astype(BF16)
 
 
-def grads_of(R, b):
+def grads_of(R, N, b):
     pick = R.pick_ch[...]
     normed = dot((R.n1, R.n2)[b][...], pick).astype(BF16)
     query_normed = dot(R.nq2[...], pick).astype(BF16) if b else normed
@@ -654,20 +652,18 @@
                 R.ga[b, q % 2, q // 2 * 2 + x_lo, y] = chunks[
                     q * CHUNK : q * CHUNK + CHUNK, x_lo * 128 : x_lo * 128 + 128
                 ]
+        core_copy(R, N, b, y).start()
 
 
 def table_of(R, b):
     R.tab[b * 8 : b * 8 + 8, :] = fold_bias(R.gb.at[b], R.offsets)
 
 
-def core_copy(R, N, b):
+def core_copy(R, N, b, y):
+    at = b * 8 + y
     return remote(
-        R.ga.at[b, 1 - N.core], R.ra.at[b], R.asend.at[b], R.arecv.at[b], N.partner()
+        R.ga.at[b, 1 - N.core, :, y], R.ra.at[b, :, y], R.asend.at[at], R.arecv.at[at], N.partner()
     )
-
-
-def start_core(R, N, b):
-    core_copy(R, N, b).start()
 
 
 def start_table(R, N):
@@ -760,7 +756,8 @@
 
 
 def start_x(R, N, b):
-    core_copy(R, N, b).wait()
+    for y in range(8):
+        core_copy(R, N, b, y).wait()
 
     over_x = x_copies(R, N, b)
     for d in (1, 3, 2, 0):
@@ -872,7 +869,7 @@
     out.update(ta=h(16, 256), rta=h(16, 256), table_out=[h(16, 256)] * 3)
     out.update(table_in=[h(4, 16, 256), h(8, 16, 256), h(8, 16, 256)])
     out.update(fsend=semaphores(8), frecv=semaphores(8), bsend=semaphores(8), brecv=semaphores(8))
-    out.update(asend=semaphores(2), arecv=semaphores(2), tsend=semaphores(1), trecv=semaphores(1))
+    out.update(asend=semaphores(16), arecv=semaphores(16), tsend=semaphores(1), trecv=semaphores(1))
     out.update(xsend=semaphores(8), xrecv=semaphores(8), ysend=semaphores(16), yrecv=semaphores(16))
     out.update(zsend=semaphores(16), zrecv=semaphores(16), tbsend=semaphores(24), tbrecv=semaphores(24))
     out.update(vsend=semaphores(16), vrecv=semaphores(16), wsend=semaphores(8), wrecv=semaphores(8))

time: 86.7 us -> 85 us (0.980); the launches traced: 86.2 us -> 83.6 us
  Pallas kernels: 85.5 us -> 82.9 us
    pallas_call x1, Pallas kernels: 83.8 us -> 81.2 us  [local(): pl.pallas_call(body, out_shape=(jax.ShapeDtypeStruct((8, 32, C), BF16), j...]
where the time goes in v4:
time: 85 us; the launch traced here: 83.6 us
  Pallas kernels  82.9 us (98%)
    pallas_call x1, Pallas kernels, local(): pl.pallas_call(body, out_shape=(jax.ShapeDtypeStruct((8, 32, C), BF16), j...  81.2 us
    pallas_call x1, Pallas kernels, local(): pl.pallas_call(hand_on, out_shape=(jax.ShapeDtypeStruct((8, 32, C), BF16)...  1.7 us

profile of v4, /device:TPU:1, one launch (start us, length us, event | category | flops | bytes accessed | tf_op | source)
XLA Modules:
  0.0 83.6 jit_solution(11375657759951388089)
XLA Ops:
  0.6 81.2 %blocks.1 = (bf16[8,32,192]{2,1,0:T(8,128)(2,1)}, f32[2,16,128]{2,1,0:T(8,128)}, f32[16,256]{1,0:T(8,128)}) custom-call(bf16[8,32,192]{2,1,0:T(8,128)(2,1)} %refs_0_.1, s32[8,32]{1,0:T(8,128)} %refs_1_.1, bf16[4,32,192]{2,1,0:T(8,128)(2,1)} %refs_2_.1, s32[4,32]{1,0:T(4,128)} %refs_3_.1, bf16[4,32,192]{2,1,0:T(8,128)(2,1)} %refs_4_.1, s32[4,32]{1,0:T(4,128)} %refs_5_.1, ...), custom_call_target="tpu_custom_call" | custom-call | tf_op jit(solution)/shard_map/blocks/pallas_call | solution.py:897
  81.9 1.7 %hand_on.1 = (bf16[8,32,192]{2,1,0:T(8,128)(2,1)}, f32[12,2,18]{2,1,0:T(2,128)}, f32[6,2,12]{2,1,0:T(2,128)}, f32[12,2,24]{2,1,0:T(2,128)}, f32[6,2,48]{2,1,0:T(2,128)}, /*index=5*/f32[6,2,225]{2,1,0:T(2,128)}) custom-call(bf16[8,32,192]{2,1,0:T(8,128)(2,1)} %get-tuple-element.15.summed, f32[2,16,128]{2,1,0:T(8,128)} %get-tuple-element.16.totals, ...), custom_call_target="tpu_custom_call" | custom-call | tf_op jit(solution)/shard_map/hand_on/pallas_call | solution.py:925
